TPU v7x, 128 devices: a whole 4x4x4 slice. The times are simulated.
128 devices in a mesh: slab: 8 (over y, z_lo), row: 4 (over z_hi, core), col: 4 (over x).
Axes of the slice: x: 4, y: 4, z: 4 (z_hi: 2, z_lo: 2; z = z_hi * 2 + z_lo), core: 2. Of those that a mesh axis runs over, the one named last changes fastest.
Arguments:
- inverse: bfloat16 [8, 8192, 4, 2048], P('slab', 'row', None, 'col'), may hold values from -0.0625 to 0.0625
- sources: bfloat16 [8, 4, 8192, 128], P('slab', None, ('row', 'col')), may hold values from -6 to 6
- coupling: float32 [8, 2, 8192], P('slab', None, ('row', 'col')), may hold values from -1 to 1
- plan: int32 [6, 8, 2], replicated, may hold values from 0 to 3
Outputs:
- up_out: bfloat16 [8, 8192, 128], P('slab', ('row', 'col'))
- down_out: bfloat16 [8, 8192, 128], P('slab', ('row', 'col'))
Inputs may be any that keep to these rules, and one draw needn't show every extreme that they name: `plan`: each entry names one of the 4 stored batches of its slab.
All inputs are finite; a program needn't handle non-finite values.
Results may differ from a plain program's by a relative error of at most 0.023.
Values may be sent and summed in bfloat16 or wider, within the bound.
No kernel may reach another device: no remote copies, remote signals or barrier semaphores. Data moves between devices by JAX's collectives and lax.ppermute only.
A program may use at most 64 MiB of HBM per device.

v0:
```python
import jax
import jax.numpy as jnp
from jax import lax
from jax.experimental import pallas as pl
from jax.experimental.pallas import tpu as pltpu
from jax.sharding import PartitionSpec as P

TICKS = 6
GROUPED = (7, 7, 7, 7, 7, 7)

VMEM = pl.BlockSpec(memory_space=pltpu.VMEM)
SMEM = pl.BlockSpec(memory_space=pltpu.SMEM)
HBM = pl.BlockSpec(memory_space=pltpu.HBM)


def f32dot(a, b):
    return jnp.dot(a, b, preferred_element_type=jnp.float32)


def wide(value):
    return value.astype(jnp.float32)


def narrow(value):
    return value.astype(jnp.bfloat16)


def shape(*lengths, kind=jnp.bfloat16):
    return jax.ShapeDtypeStruct(lengths, kind)


def call(kernel, outs, *args, specs=None, scratch=(), limit=24 << 20):
    return pl.pallas_call(
        kernel,
        out_shape=outs,
        in_specs=specs or [VMEM] * len(args),
        out_specs=jax.tree.map(lambda _: VMEM, outs),
        scratch_shapes=scratch,
        compiler_params=pltpu.CompilerParams(vmem_limit_bytes=limit),
    )(*args)


def place_kernel(source, out, buffer, sem):
    row, col = lax.axis_index("row"), lax.axis_index("col")
    core = row % 2
    near = (row // 2 + core) % 2
    chunk = buffer.shape[1]
    count = buffer.shape[0]
    per_piece = out.shape[2] // chunk

    def copy(i):
        return pltpu.make_async_copy(source.at[pl.ds(i * chunk, chunk)], buffer.at[i], sem.at[i])

    for i in range(count):
        copy(i).start()

    def step(i, carry):
        copy(i).wait()
        turned = jnp.swapaxes(buffer[i], 0, 1)
        m = (i // per_piece - col + 4) % 4
        for k in range(4):
            same = (core + k) % 2
            j = jnp.where(k // 2 == near, same, 3 - same)
            out[m, j, pl.ds((i % per_piece) * chunk, chunk), :] = turned[k]
        return carry

    lax.fori_loop(0, count, step, 0)


def first_kernel(plan, stored, up, down, after):
    slab = lax.axis_index("slab")
    up[...] = stored[plan[0, 0, slab]]
    down[...] = narrow(wide(stored[plan[0, 1, slab]]).T)
    after[0] = stored[plan[1, 0, slab]]
    after[1] = stored[plan[2, 0, slab]]


def spread_kernel(gain, out):
    row_gain = jnp.where(lax.axis_index("slab") == 7, 0.0, gain[...])
    out[...] = jnp.broadcast_to(row_gain, (out.shape[1], out.shape[0])).T


def pick_up_kernel(plan, stored, out):
    slab = lax.axis_index("slab")
    for t in range(3, TICKS):
        out[t - 3] = stored[plan[t, 0, slab]]


def pick_down_kernel(plan, stored, out):
    slab = lax.axis_index("slab")

    def step(t, carry):
        out[t] = narrow(wide(stored[plan[t + 1, 1, slab]]).T)
        return carry

    lax.fori_loop(0, TICKS - 1, step, 0)


def stack_kernel(own, other, out):
    out[0] = own[...]
    out[1] = other[...]


def up_first_kernel(blocks, x, acc):
    def step(m, carry):
        acc[m] = f32dot(blocks[m, 0], x[0]) + f32dot(blocks[m, 1], x[1])
        return carry

    lax.fori_loop(0, 4, step, 0, unroll=2)


def up_last_kernel(blocks, x, acc, out):
    def step(m, carry):
        out[m] = narrow(acc[m] + f32dot(blocks[m, 2], x[0]) + f32dot(blocks[m, 3], x[1]))
        return carry

    lax.fori_loop(0, 4, step, 0)


def up_sum_kernel(own, p1, p2, p3, out):
    out[...] = narrow(wide(own[0]) + wide(p1[...]) + wide(p2[...]) + wide(p3[...]))


def up_next_kernel(t, own, p1, p2, p3, source, gain, out):
    carried = narrow(wide(own[0]) + wide(p1[...]) + wide(p2[...]) + wide(p3[...]))
    chosen = source[t if t < 2 else t - 2]
    out[...] = narrow(wide(chosen) + gain[...] * wide(carried))


def down_first_kernel(blocks, x0, acc):
    def step(j, carry):
        acc[j] = f32dot(x0[...], blocks[0, j])
        return carry

    lax.fori_loop(0, 4, step, 0)


def down_more_kernel(blocks, x1, x2, acc, out):
    def step(j, carry):
        out[j] = acc[j] + f32dot(x1[...], blocks[1, j]) + f32dot(x2[...], blocks[2, j])
        return carry

    lax.fori_loop(0, 4, step, 0, unroll=2)


def down_last_kernel(blocks, x3, acc, kept, sent):
    def step(j, carry):
        sent[j] = narrow(acc[2 + j] + f32dot(x3[...], blocks[3, 2 + j]))
        kept[j] = acc[j] + f32dot(x3[...], blocks[3, j])
        return carry

    lax.fori_loop(0, 2, step, 0)


def down_pair_kernel(kept, got, out):
    out[...] = narrow(kept[...] + wide(got[...]))


def down_next_kernel(t, moved, got, source, gain, out):
    carried = narrow(wide(moved[0]) + wide(got[...]))
    used = jnp.where(lax.axis_index("slab") == 7, 0.0, gain[...])
    out[...] = narrow(wide(source[t]) + used * wide(carried))


def down_sum_kernel(moved, got, out):
    out[...] = narrow((wide(moved[0]) + wide(got[...])).T)


def per_device(inverse, sources, coupling, plan):
    slabs, rows, cols = (lax.axis_size(a) for a in ("slab", "row", "col"))
    piece, width = sources.shape[2:]
    top = slabs - 1
    everyone = list(range(slabs))

    def swap_cores(value, active):
        pairs = [(s * rows + r, s * rows + (r ^ 1)) for s in active for r in range(rows)]
        return lax.ppermute(value, ("slab", "row"), pairs)

    def target(r):
        return r ^ 2 if r % 2 else r

    def over_slab(value, active, step):
        pairs = [(s * rows + r, ((s + step) % slabs) * rows + target(r)) for s in active for r in range(rows)]
        return lax.ppermute(value, ("slab", "row"), pairs)

    def over_half(value, active):
        pairs = [(s * rows + r, s * rows + target(r)) for s in active for r in range(rows)]
        return lax.ppermute(value, ("slab", "row"), pairs)

    def over_col(value, active, step):
        pairs = [(s * cols + c, s * cols + (c + step) % cols) for s in active for c in range(cols)]
        return lax.ppermute(value, ("slab", "col"), pairs)

    stored = sources[0]
    plan = jnp.swapaxes(plan, 1, 2)
    down_gain = coupling[0, 1][None, :]
    piece_u = shape(piece, width)
    piece_d = shape(width, piece)
    pair_u = shape(2, piece, width)
    pair_d = shape(2, width, piece)
    kept_d = shape(2, width, piece, kind=jnp.float32)
    acc_up = shape(cols, piece, width, kind=jnp.float32)
    acc_down = shape(rows, width, piece, kind=jnp.float32)
    up_in, down_in, after = call(first_kernel, (piece_u, piece_d, pair_u), plan, stored, specs=[SMEM, VMEM])
    shift_pairs = [(s * rows + r, ((s - 1) % slabs) * rows + r) for s in everyone for r in range(rows)]
    next_source = lax.ppermute(after, ("slab", "row"), shift_pairs)
    later = call(pick_up_kernel, shape(TICKS - 3, piece, width), plan, stored, specs=[SMEM, VMEM])
    later = lax.ppermute(later, ("slab", "row"), shift_pairs)
    next_gain = lax.ppermute(coupling[0, 0], ("slab", "row"), shift_pairs)[None, :]
    blocks = call(
        place_kernel,
        shape(cols, rows, piece, piece),
        inverse[0],
        specs=[HBM],
        scratch=[pltpu.VMEM((8, 256, rows, piece), jnp.bfloat16), pltpu.SemaphoreType.DMA((8,))],
        limit=40 << 20,
    )
    up_gain = call(spread_kernel, shape(piece, width, kind=jnp.float32), next_gain)
    down_sources = call(pick_down_kernel, shape(TICKS - 1, width, piece), plan, stored, specs=[SMEM, VMEM])
    for t in range(TICKS):
        last = t == TICKS - 1
        up_on = [s for s in range(slabs) if s <= GROUPED[t]]
        down_on = [s for s in range(slabs) if s >= top - GROUPED[t]]
        senders = up_on if t == 0 else [(s - 1) % slabs for s in up_on]

        d2 = over_col(down_in, down_on, -2)
        d1 = over_col(down_in, down_on, -1)
        d3 = over_col(down_in, down_on, -3)
        other = swap_cores(up_in, senders)
        acc_d = call(down_first_kernel, acc_down, blocks, down_in)
        pair = call(stack_kernel, pair_u, up_in, other)
        if t == 0:
            moved = over_half(pair, up_on)
        else:
            moved = over_slab(pair, senders, 1)
        acc_d = call(down_more_kernel, acc_down, blocks, d1, d2, acc_d)
        kept, sent = call(down_last_kernel, (kept_d, pair_d), blocks, d3, acc_d)
        got = swap_cores(sent, down_on)
        other = swap_cores(moved, up_on)
        acc_u = call(up_first_kernel, acc_up, blocks, moved)
        pair = call(down_pair_kernel, pair_d, kept, got)
        if last:
            moved_d = over_half(pair, down_on)
        else:
            moved_d = over_slab(pair, down_on, -1)
        made = call(up_last_kernel, shape(cols, piece, width), blocks, other, acc_u)
        parts = [made] + [over_col(made[m], up_on, m) for m in (1, 2, 3)]
        got = swap_cores(moved_d[1], down_on)
        if last:
            up_out = call(up_sum_kernel, piece_u, parts[0], parts[1], parts[2], parts[3])
            down_out = call(down_sum_kernel, piece_u, moved_d, got)
        else:
            down_in = call(
                lambda *refs, t=t: down_next_kernel(t, *refs), piece_d, moved_d, got, down_sources, down_gain
            )
            up_in = call(
                lambda *refs, t=t: up_next_kernel(t, *refs),
                piece_u,
                parts[0],
                parts[1],
                parts[2],
                parts[3],
                later if t > 1 else next_source,
                up_gain,
            )
    return (up_out[None], down_out[None])


def solution(mesh):
    placed = (
        P("slab", "row", None, "col"),
        P("slab", None, ("row", "col"), None),
        P("slab", None, ("row", "col")),
        P(),
    )
    return jax.shard_map(
        per_device,
        mesh=mesh,
        in_specs=placed,
        out_specs=(P("slab", ("row", "col"), None), P("slab", ("row", "col"), None)),
        check_vma=False,
    )
```

profile of v0, /device:TPU:1, one launch (start us, length us, event | category | flops | bytes accessed | tf_op | source)
XLA Modules:
  0.0 209.9 jit_solution(12895386808371772704)
XLA Ops:
  3.1 1.5 collective-permute-start
  5.6 5.6 %collective-permute-start.1 = (bf16[2,512,128]{2,1,0:T(8,128)(2,1)S(1)}, bf16[2,512,128]{2,1,0:T(8,128)(2,1)S(1)}, u32[]{:S(2)}, u32[]{:S(2)}) collective-permute-start(bf16[2,512,128]{2,1,0:T(8,128)(2,1)S(1)} %shard_map.61), channel_id=1, source_target_pairs={{0,0},{4,12},{8,8},{12,4},{16,16},{20,28},{24,24},{28,20},{32,32},... | collective-permute-start | bytes 786440 | tf_op jit(solution)/shard_map/ppermute | solution.py:188
  11.2 2.5 %collective-permute-start.40 = (bf16[128,512]{1,0:T(8,128)(2,1)S(1)}, bf16[128,512]{1,0:T(8,128)(2,1)S(1)}, u32[]{:S(2)}, u32[]{:S(2)}) collective-permute-start(bf16[128,512]{1,0:T(8,128)(2,1)S(1)} %get-tuple-element.19.x0), channel_id=1, source_target_pairs={{0,3},{1,0},{2,1},{3,2},{16,19},{17,16},{18,17},{19,18},{32,35},{3... | collective-permute-start | bytes 393224 | tf_op jit(solution)/shard_map/ppermute | solution.py:192
  14.9 3.7 %shard_map.59.blocks = bf16[4,4,512,512]{3,2,1,0:T(8,128)(2,1)S(1)} custom-call(bf16[2048,4,512]{2,1,0:T(4,128)(2,1)} %bitcast.64), custom_call_target="tpu_custom_call" | custom-call | tf_op jit(solution)/shard_map/pallas_call | solution.py:33
  21.7 3.2 %collective-permute-start.6 = (bf16[2,512,128]{2,1,0:T(8,128)(2,1)S(1)}, bf16[2,512,128]{2,1,0:T(8,128)(2,1)S(1)}, u32[]{:S(2)}, u32[]{:S(2)}) collective-permute-start(bf16[2,512,128]{2,1,0:T(8,128)(2,1)S(1)} %get-tuple-element.18), channel_id=1, source_target_pairs={{0,112},{4,116},{8,120},{12,124},{16,0},{20,4},{24,8},{28,12},{32,... | collective-permute-start | bytes 786440 | tf_op jit(solution)/shard_map/ppermute | solution.py:206
  25.8 3.4 %collective-permute-start.43 = (bf16[2,128,512]{2,1,0:T(8,128)(2,1)S(1)}, bf16[2,128,512]{2,1,0:T(8,128)(2,1)S(1)}, u32[]{:S(2)}, u32[]{:S(2)}) collective-permute-start(bf16[2,128,512]{2,1,0:T(8,128)(2,1)S(1)} %shard_map.90), channel_id=1, source_target_pairs={{0,112},{4,124},{8,120},{12,116},{16,0},{20,12},{24,8},{28,4},{32,... | collective-permute-start | bytes 786440 | tf_op jit(solution)/shard_map/ppermute | solution.py:184
  29.1 1.4 shard_map.62.acc
  30.6 1.8 shard_map.63.refs_0_
  32.5 1.2 collective-permute-start.4
  33.7 1.4 collective-permute-start.5
  35.3 5.4 %collective-permute-done.3.refs_1_ = bf16[512,128]{1,0:T(8,128)(2,1)S(1)} collective-permute-done((bf16[512,128]{1,0:T(8,128)(2,1)S(1)}, bf16[512,128]{1,0:T(8,128)(2,1)S(1)}, u32[]{:S(2)}, u32[]{:S(2)}) %collective-permute-start.3) | collective-permute-done | bytes 131104 | tf_op jit(solution)/shard_map/ppermute | solution.py:192
  44.1 1.2 shard_map.91.refs_2_
  45.4 2.5 %collective-permute-start.46 = (bf16[128,512]{1,0:T(8,128)(2,1)S(1)}, bf16[128,512]{1,0:T(8,128)(2,1)S(1)}, u32[]{:S(2)}, u32[]{:S(2)}) collective-permute-start(bf16[128,512]{1,0:T(8,128)(2,1)S(1)} %shard_map.92.x0), channel_id=1, source_target_pairs={{0,3},{1,0},{2,1},{3,2},{16,19},{17,16},{18,17},{19,18},{32,35},{3... | collective-permute-start | bytes 393224 | tf_op jit(solution)/shard_map/ppermute | solution.py:192
  49.4 4.1 %collective-permute-done.46.x1 = bf16[128,512]{1,0:T(8,128)(2,1)S(1)} collective-permute-done((bf16[128,512]{1,0:T(8,128)(2,1)S(1)}, bf16[128,512]{1,0:T(8,128)(2,1)S(1)}, u32[]{:S(2)}, u32[]{:S(2)}) %collective-permute-start.46) | collective-permute-done | bytes 131104 | tf_op jit(solution)/shard_map/ppermute | solution.py:192
  55.2 2.2 %collective-permute-done.45.x3 = bf16[128,512]{1,0:T(8,128)(2,1)S(1)} collective-permute-done((bf16[128,512]{1,0:T(8,128)(2,1)S(1)}, bf16[128,512]{1,0:T(8,128)(2,1)S(1)}, u32[]{:S(2)}, u32[]{:S(2)}) %collective-permute-start.45) | collective-permute-done | bytes 131104 | tf_op jit(solution)/shard_map/ppermute | solution.py:192
  58.8 1.1 collective-permute-done.48.got
  59.9 4.1 %collective-permute-start.49 = (bf16[2,128,512]{2,1,0:T(8,128)(2,1)S(1)}, bf16[2,128,512]{2,1,0:T(8,128)(2,1)S(1)}, u32[]{:S(2)}, u32[]{:S(2)}) collective-permute-start(bf16[2,128,512]{2,1,0:T(8,128)(2,1)S(1)} %shard_map.96), channel_id=1, source_target_pairs={{0,112},{4,124},{8,120},{12,116},{16,0},{20,12},{24,8},{28,4},{32,... | collective-permute-start | bytes 786440 | tf_op jit(solution)/shard_map/ppermute | solution.py:184
  64.0 1.4 shard_map.67.acc
  65.5 1.8 shard_map.68.refs_0_
  67.4 1.6 collective-permute-start.12
  69.0 1.1 collective-permute-start.13
  70.0 5.6 %collective-permute-done.11.refs_1_ = bf16[512,128]{1,0:T(8,128)(2,1)S(1)} collective-permute-done((bf16[512,128]{1,0:T(8,128)(2,1)S(1)}, bf16[512,128]{1,0:T(8,128)(2,1)S(1)}, u32[]{:S(2)}, u32[]{:S(2)}) %collective-permute-start.11) | collective-permute-done | bytes 131104 | tf_op jit(solution)/shard_map/ppermute | solution.py:192
  78.5 2.3 %collective-permute-start.52 = (bf16[128,512]{1,0:T(8,128)(2,1)S(1)}, bf16[128,512]{1,0:T(8,128)(2,1)S(1)}, u32[]{:S(2)}, u32[]{:S(2)}) collective-permute-start(bf16[128,512]{1,0:T(8,128)(2,1)S(1)} %shard_map.97.x0), channel_id=1, source_target_pairs={{0,3},{1,0},{2,1},{3,2},{16,19},{17,16},{18,17},{19,18},{32,35},{3... | collective-permute-start | bytes 393224 | tf_op jit(solution)/shard_map/ppermute | solution.py:192
  82.5 1.7 collective-permute-done.52.x1
  84.2 2.8 %collective-permute-done.53.x2 = bf16[128,512]{1,0:T(8,128)(2,1)S(1)} collective-permute-done((bf16[128,512]{1,0:T(8,128)(2,1)S(1)}, bf16[128,512]{1,0:T(8,128)(2,1)S(1)}, u32[]{:S(2)}, u32[]{:S(2)}) %collective-permute-start.53) | collective-permute-done | bytes 131104 | tf_op jit(solution)/shard_map/ppermute | solution.py:192
  87.9 2.1 %collective-permute-done.51.x3 = bf16[128,512]{1,0:T(8,128)(2,1)S(1)} collective-permute-done((bf16[128,512]{1,0:T(8,128)(2,1)S(1)}, bf16[128,512]{1,0:T(8,128)(2,1)S(1)}, u32[]{:S(2)}, u32[]{:S(2)}) %collective-permute-start.51) | collective-permute-done | bytes 131104 | tf_op jit(solution)/shard_map/ppermute | solution.py:192
  92.3 2.2 %collective-permute-start.20 = (bf16[3,512,128]{2,1,0:T(8,128)(2,1)S(1)}, bf16[3,512,128]{2,1,0:T(8,128)(2,1)S(1)}, u32[]{:S(2)}, u32[]{:S(2)}) collective-permute-start(bf16[3,512,128]{2,1,0:T(8,128)(2,1)S(1)} %shard_map.73), channel_id=1, source_target_pairs={{0,112},{4,116},{8,120},{12,124},{16,0},{20,4},{24,8},{28,12},{32,... | collective-permute-start | bytes 1179656 | tf_op jit(solution)/shard_map/ppermute | solution.py:208
  94.5 2.6 %collective-permute-start.55 = (bf16[2,128,512]{2,1,0:T(8,128)(2,1)S(1)}, bf16[2,128,512]{2,1,0:T(8,128)(2,1)S(1)}, u32[]{:S(2)}, u32[]{:S(2)}) collective-permute-start(bf16[2,128,512]{2,1,0:T(8,128)(2,1)S(1)} %shard_map.101), channel_id=1, source_target_pairs={{0,112},{4,124},{8,120},{12,116},{16,0},{20,12},{24,8},{28,4},{32,... | collective-permute-start | bytes 786440 | tf_op jit(solution)/shard_map/ppermute | solution.py:184
  97.1 1.4 shard_map.71.acc
  98.5 1.8 shard_map.72.refs_0_
  100.4 1.3 collective-permute-start.18
  101.7 1.3 collective-permute-start.19
  103.0 5.5 %collective-permute-done.17.refs_1_ = bf16[512,128]{1,0:T(8,128)(2,1)S(1)} collective-permute-done((bf16[512,128]{1,0:T(8,128)(2,1)S(1)}, bf16[512,128]{1,0:T(8,128)(2,1)S(1)}, u32[]{:S(2)}, u32[]{:S(2)}) %collective-permute-start.17) | collective-permute-done | bytes 131104 | tf_op jit(solution)/shard_map/ppermute | solution.py:192
  111.0 1.4 collective-permute-start.22
  112.5 2.1 collective-permute-start.58
  116.2 1.4 collective-permute-done.58.x1
  117.6 2.6 %collective-permute-done.59.x2 = bf16[128,512]{1,0:T(8,128)(2,1)S(1)} collective-permute-done((bf16[128,512]{1,0:T(8,128)(2,1)S(1)}, bf16[128,512]{1,0:T(8,128)(2,1)S(1)}, u32[]{:S(2)}, u32[]{:S(2)}) %collective-permute-start.59) | collective-permute-done | bytes 131104 | tf_op jit(solution)/shard_map/ppermute | solution.py:192
  121.1 2.6 %collective-permute-done.57.x3 = bf16[128,512]{1,0:T(8,128)(2,1)S(1)} collective-permute-done((bf16[128,512]{1,0:T(8,128)(2,1)S(1)}, bf16[128,512]{1,0:T(8,128)(2,1)S(1)}, u32[]{:S(2)}, u32[]{:S(2)}) %collective-permute-start.57) | collective-permute-done | bytes 131104 | tf_op jit(solution)/shard_map/ppermute | solution.py:192
  125.3 1.1 collective-permute-done.60.got
  126.4 3.8 %collective-permute-start.61 = (bf16[2,128,512]{2,1,0:T(8,128)(2,1)S(1)}, bf16[2,128,512]{2,1,0:T(8,128)(2,1)S(1)}, u32[]{:S(2)}, u32[]{:S(2)}) collective-permute-start(bf16[2,128,512]{2,1,0:T(8,128)(2,1)S(1)} %shard_map.106), channel_id=1, source_target_pairs={{0,112},{4,124},{8,120},{12,116},{16,0},{20,12},{24,8},{28,4},{32,... | collective-permute-start | bytes 786440 | tf_op jit(solution)/shard_map/ppermute | solution.py:184
  130.2 1.4 shard_map.76.acc
  131.6 1.8 shard_map.77.refs_0_
  133.5 2.1 collective-permute-start.25
  136.2 6.6 %collective-permute-done.24.refs_1_ = bf16[512,128]{1,0:T(8,128)(2,1)S(1)} collective-permute-done((bf16[512,128]{1,0:T(8,128)(2,1)S(1)}, bf16[512,128]{1,0:T(8,128)(2,1)S(1)}, u32[]{:S(2)}, u32[]{:S(2)}) %collective-permute-start.24) | collective-permute-done | bytes 131104 | tf_op jit(solution)/shard_map/ppermute | solution.py:192
  145.8 2.3 %collective-permute-start.64 = (bf16[128,512]{1,0:T(8,128)(2,1)S(1)}, bf16[128,512]{1,0:T(8,128)(2,1)S(1)}, u32[]{:S(2)}, u32[]{:S(2)}) collective-permute-start(bf16[128,512]{1,0:T(8,128)(2,1)S(1)} %shard_map.107.x0), channel_id=1, source_target_pairs={{0,3},{1,0},{2,1},{3,2},{16,19},{17,16},{18,17},{19,18},{32,35},{3... | collective-permute-start | bytes 393224 | tf_op jit(solution)/shard_map/ppermute | solution.py:192
  149.7 1.5 collective-permute-done.64.x1
  151.2 3.1 %collective-permute-done.65.x2 = bf16[128,512]{1,0:T(8,128)(2,1)S(1)} collective-permute-done((bf16[128,512]{1,0:T(8,128)(2,1)S(1)}, bf16[128,512]{1,0:T(8,128)(2,1)S(1)}, u32[]{:S(2)}, u32[]{:S(2)}) %collective-permute-start.65) | collective-permute-done | bytes 131104 | tf_op jit(solution)/shard_map/ppermute | solution.py:192
  155.2 2.1 collective-permute-done.63.x3
  158.9 1.1 collective-permute-done.66.got
  160.0 3.7 %collective-permute-start.67 = (bf16[2,128,512]{2,1,0:T(8,128)(2,1)S(1)}, bf16[2,128,512]{2,1,0:T(8,128)(2,1)S(1)}, u32[]{:S(2)}, u32[]{:S(2)}) collective-permute-start(bf16[2,128,512]{2,1,0:T(8,128)(2,1)S(1)} %shard_map.111), channel_id=1, source_target_pairs={{0,112},{4,124},{8,120},{12,116},{16,0},{20,12},{24,8},{28,4},{32,... | collective-permute-start | bytes 786440 | tf_op jit(solution)/shard_map/ppermute | solution.py:184
  163.7 1.4 shard_map.80.acc
  165.1 1.8 shard_map.81.refs_0_
  167.0 1.8 collective-permute-start.31
  169.7 6.0 %collective-permute-done.30.refs_1_ = bf16[512,128]{1,0:T(8,128)(2,1)S(1)} collective-permute-done((bf16[512,128]{1,0:T(8,128)(2,1)S(1)}, bf16[512,128]{1,0:T(8,128)(2,1)S(1)}, u32[]{:S(2)}, u32[]{:S(2)}) %collective-permute-start.30) | collective-permute-done | bytes 131104 | tf_op jit(solution)/shard_map/ppermute | solution.py:192
  178.7 2.4 %collective-permute-start.70 = (bf16[128,512]{1,0:T(8,128)(2,1)S(1)}, bf16[128,512]{1,0:T(8,128)(2,1)S(1)}, u32[]{:S(2)}, u32[]{:S(2)}) collective-permute-start(bf16[128,512]{1,0:T(8,128)(2,1)S(1)} %shard_map.112.x0), channel_id=1, source_target_pairs={{0,3},{1,0},{2,1},{3,2},{16,19},{17,16},{18,17},{19,18},{32,35},{3... | collective-permute-start | bytes 393224 | tf_op jit(solution)/shard_map/ppermute | solution.py:192
  182.6 3.8 %collective-permute-done.70.x1 = bf16[128,512]{1,0:T(8,128)(2,1)S(1)} collective-permute-done((bf16[128,512]{1,0:T(8,128)(2,1)S(1)}, bf16[128,512]{1,0:T(8,128)(2,1)S(1)}, u32[]{:S(2)}, u32[]{:S(2)}) %collective-permute-start.70) | collective-permute-done | bytes 131104 | tf_op jit(solution)/shard_map/ppermute | solution.py:192
  188.1 2.1 collective-permute-done.69.x3
  191.8 1.1 collective-permute-done.72.got
  192.9 2.4 %collective-permute-start.73 = (bf16[2,128,512]{2,1,0:T(8,128)(2,1)S(1)}, bf16[2,128,512]{2,1,0:T(8,128)(2,1)S(1)}, u32[]{:S(2)}, u32[]{:S(2)}) collective-permute-start(bf16[2,128,512]{2,1,0:T(8,128)(2,1)S(1)} %shard_map.116), channel_id=1, source_target_pairs={{0,0},{4,12},{8,8},{12,4},{16,16},{20,28},{24,24},{28,20},{32,32},... | collective-permute-start | bytes 786440 | tf_op jit(solution)/shard_map/ppermute | solution.py:188
  195.3 1.4 shard_map.84.acc
  196.7 1.8 shard_map.85.own
  198.6 2.9 %collective-permute-done.73.moved = bf16[2,128,512]{2,1,0:T(8,128)(2,1)S(1)} collective-permute-done((bf16[2,128,512]{2,1,0:T(8,128)(2,1)S(1)}, bf16[2,128,512]{2,1,0:T(8,128)(2,1)S(1)}, u32[]{:S(2)}, u32[]{:S(2)}) %collective-permute-start.73) | collective-permute-done | bytes 262176 | tf_op jit(solution)/shard_map/ppermute | solution.py:188
  204.1 3.7 %collective-permute-done.37.p2 = bf16[512,128]{1,0:T(8,128)(2,1)S(1)} collective-permute-done((bf16[512,128]{1,0:T(8,128)(2,1)S(1)}, bf16[512,128]{1,0:T(8,128)(2,1)S(1)}, u32[]{:S(2)}, u32[]{:S(2)}) %collective-permute-start.37) | collective-permute-done | bytes 131104 | tf_op jit(solution)/shard_map/ppermute | solution.py:192
  207.8 1.4 collective-permute-done.38.p3
  (168 shorter events, 51.5 us)
Async XLA Ops:
  3.1 2.4 %collective-permute-start = (bf16[512,128]{1,0:T(8,128)(2,1)S(1)}, bf16[512,128]{1,0:T(8,128)(2,1)S(1)}, u32[]{:S(2)}, u32[]{:S(2)}) collective-permute-start(bf16[512,128]{1,0:T(8,128)(2,1)S(1)} %get-tuple-element.17.own), channel_id=1, source_target_pairs={{0,4},{4,0},{8,12},{12,8},{16,20},{20,16},{24,28},{28,24},{32,36},... | collective-permute-start | bytes 393224 | tf_op jit(solution)/shard_map/ppermute | solution.py:177
  5.6 15.6 %collective-permute-start.1 = (bf16[2,512,128]{2,1,0:T(8,128)(2,1)S(1)}, bf16[2,512,128]{2,1,0:T(8,128)(2,1)S(1)}, u32[]{:S(2)}, u32[]{:S(2)}) collective-permute-start(bf16[2,512,128]{2,1,0:T(8,128)(2,1)S(1)} %shard_map.61), channel_id=1, source_target_pairs={{0,0},{4,12},{8,8},{12,4},{16,16},{20,28},{24,24},{28,20},{32,32},... | collective-permute-start | bytes 786440 | tf_op jit(solution)/shard_map/ppermute | solution.py:188
  11.2 8.3 %collective-permute-start.40 = (bf16[128,512]{1,0:T(8,128)(2,1)S(1)}, bf16[128,512]{1,0:T(8,128)(2,1)S(1)}, u32[]{:S(2)}, u32[]{:S(2)}) collective-permute-start(bf16[128,512]{1,0:T(8,128)(2,1)S(1)} %get-tuple-element.19.x0), channel_id=1, source_target_pairs={{0,3},{1,0},{2,1},{3,2},{16,19},{17,16},{18,17},{19,18},{32,35},{3... | collective-permute-start | bytes 393224 | tf_op jit(solution)/shard_map/ppermute | solution.py:192
  13.8 5.8 %collective-permute-start.41 = (bf16[128,512]{1,0:T(8,128)(2,1)S(1)}, bf16[128,512]{1,0:T(8,128)(2,1)S(1)}, u32[]{:S(2)}, u32[]{:S(2)}) collective-permute-start(bf16[128,512]{1,0:T(8,128)(2,1)S(1)} %get-tuple-element.19.x0), channel_id=1, source_target_pairs={{0,2},{1,3},{2,0},{3,1},{16,18},{17,19},{18,16},{19,17},{32,34},{3... | collective-permute-start | bytes 393224 | tf_op jit(solution)/shard_map/ppermute | solution.py:192
  14.3 6.2 %collective-permute-start.39 = (bf16[128,512]{1,0:T(8,128)(2,1)S(1)}, bf16[128,512]{1,0:T(8,128)(2,1)S(1)}, u32[]{:S(2)}, u32[]{:S(2)}) collective-permute-start(bf16[128,512]{1,0:T(8,128)(2,1)S(1)} %get-tuple-element.19.x0), channel_id=1, source_target_pairs={{0,1},{1,2},{2,3},{3,0},{16,17},{17,18},{18,19},{19,16},{32,33},{3... | collective-permute-start | bytes 393224 | tf_op jit(solution)/shard_map/ppermute | solution.py:192
  21.1 4.6 %collective-permute-start.42 = (bf16[2,128,512]{2,1,0:T(8,128)(2,1)S(1)}, bf16[2,128,512]{2,1,0:T(8,128)(2,1)S(1)}, u32[]{:S(2)}, u32[]{:S(2)}) collective-permute-start(bf16[2,128,512]{2,1,0:T(8,128)(2,1)S(1)} %get-tuple-element.21), channel_id=1, source_target_pairs={{0,4},{4,0},{8,12},{12,8},{16,20},{20,16},{24,28},{28,24},{32,36},... | collective-permute-start | bytes 786440 | tf_op jit(solution)/shard_map/ppermute | solution.py:177
  21.2 9.3 %collective-permute-start.2 = (bf16[2,512,128]{2,1,0:T(8,128)(2,1)S(1)}, bf16[2,512,128]{2,1,0:T(8,128)(2,1)S(1)}, u32[]{:S(2)}, u32[]{:S(2)}) collective-permute-start(bf16[2,512,128]{2,1,0:T(8,128)(2,1)S(1)} %collective-permute-done.1.x), channel_id=1, source_target_pairs={{0,4},{4,0},{8,12},{12,8},{16,20},{20,16},{24,28},{28,24},{32,36},... | collective-permute-start | bytes 786440 | tf_op jit(solution)/shard_map/ppermute | solution.py:177
  21.7 13.6 %collective-permute-start.6 = (bf16[2,512,128]{2,1,0:T(8,128)(2,1)S(1)}, bf16[2,512,128]{2,1,0:T(8,128)(2,1)S(1)}, u32[]{:S(2)}, u32[]{:S(2)}) collective-permute-start(bf16[2,512,128]{2,1,0:T(8,128)(2,1)S(1)} %get-tuple-element.18), channel_id=1, source_target_pairs={{0,112},{4,116},{8,120},{12,124},{16,0},{20,4},{24,8},{28,12},{32,... | collective-permute-start | bytes 786440 | tf_op jit(solution)/shard_map/ppermute | solution.py:206
  24.9 8.8 %collective-permute-start.7 = (f32[512]{0:T(512)S(1)}, f32[512]{0:T(512)S(1)}, u32[]{:S(2)}, u32[]{:S(2)}) collective-permute-start(f32[512]{0:T(512)S(1)} %bitcast.67), channel_id=1, source_target_pairs={{0,112},{4,116},{8,120},{12,124},{16,0},{20,4},{24,8},{28,12},{32,... | collective-permute-start | bytes 6152 | tf_op jit(solution)/shard_map/ppermute | solution.py:209
  25.8 16.0 %collective-permute-start.43 = (bf16[2,128,512]{2,1,0:T(8,128)(2,1)S(1)}, bf16[2,128,512]{2,1,0:T(8,128)(2,1)S(1)}, u32[]{:S(2)}, u32[]{:S(2)}) collective-permute-start(bf16[2,128,512]{2,1,0:T(8,128)(2,1)S(1)} %shard_map.90), channel_id=1, source_target_pairs={{0,112},{4,124},{8,120},{12,116},{16,0},{20,12},{24,8},{28,4},{32,... | collective-permute-start | bytes 786440 | tf_op jit(solution)/shard_map/ppermute | solution.py:184
  32.4 8.3 %collective-permute-start.3 = (bf16[512,128]{1,0:T(8,128)(2,1)S(1)}, bf16[512,128]{1,0:T(8,128)(2,1)S(1)}, u32[]{:S(2)}, u32[]{:S(2)}) collective-permute-start(bf16[512,128]{1,0:T(8,128)(2,1)S(1)} %get-tuple-element.49), channel_id=1, source_target_pairs={{0,1},{1,2},{2,3},{3,0},{16,17},{17,18},{18,19},{19,16},{32,33},{3... | collective-permute-start | bytes 393224 | tf_op jit(solution)/shard_map/ppermute | solution.py:192
  32.5 8.2 %collective-permute-start.4 = (bf16[512,128]{1,0:T(8,128)(2,1)S(1)}, bf16[512,128]{1,0:T(8,128)(2,1)S(1)}, u32[]{:S(2)}, u32[]{:S(2)}) collective-permute-start(bf16[512,128]{1,0:T(8,128)(2,1)S(1)} %get-tuple-element.48), channel_id=1, source_target_pairs={{0,2},{1,3},{2,0},{3,1},{16,18},{17,19},{18,16},{19,17},{32,34},{3... | collective-permute-start | bytes 393224 | tf_op jit(solution)/shard_map/ppermute | solution.py:192
  33.7 7.9 %collective-permute-start.5 = (bf16[512,128]{1,0:T(8,128)(2,1)S(1)}, bf16[512,128]{1,0:T(8,128)(2,1)S(1)}, u32[]{:S(2)}, u32[]{:S(2)}) collective-permute-start(bf16[512,128]{1,0:T(8,128)(2,1)S(1)} %get-tuple-element.47), channel_id=1, source_target_pairs={{0,3},{1,0},{2,1},{3,2},{16,19},{17,16},{18,17},{19,18},{32,35},{3... | collective-permute-start | bytes 393224 | tf_op jit(solution)/shard_map/ppermute | solution.py:192
  41.8 3.4 %collective-permute-start.44 = (bf16[128,512]{1,0:T(8,128)(2,1)S(1)}, bf16[128,512]{1,0:T(8,128)(2,1)S(1)}, u32[]{:S(2)}, u32[]{:S(2)}) collective-permute-start(bf16[128,512]{1,0:T(8,128)(2,1)S(1)} %slice_bitcast_fusion.5), channel_id=1, source_target_pairs={{0,4},{4,0},{8,12},{12,8},{16,20},{20,16},{24,28},{28,24},{32,36},... | collective-permute-start | bytes 393224 | tf_op jit(solution)/shard_map/ppermute | solution.py:177
  43.2 15.5 %collective-permute-start.9 = (bf16[2,512,128]{2,1,0:T(8,128)(2,1)S(1)}, bf16[2,512,128]{2,1,0:T(8,128)(2,1)S(1)}, u32[]{:S(2)}, u32[]{:S(2)}) collective-permute-start(bf16[2,512,128]{2,1,0:T(8,128)(2,1)S(1)} %shard_map.66), channel_id=1, source_target_pairs={{112,0},{116,12},{120,8},{124,4},{0,16},{4,28},{8,24},{12,20},{16,... | collective-permute-start | bytes 786440 | tf_op jit(solution)/shard_map/ppermute | solution.py:184
  45.4 8.1 %collective-permute-start.46 = (bf16[128,512]{1,0:T(8,128)(2,1)S(1)}, bf16[128,512]{1,0:T(8,128)(2,1)S(1)}, u32[]{:S(2)}, u32[]{:S(2)}) collective-permute-start(bf16[128,512]{1,0:T(8,128)(2,1)S(1)} %shard_map.92.x0), channel_id=1, source_target_pairs={{0,3},{1,0},{2,1},{3,2},{16,19},{17,16},{18,17},{19,18},{32,35},{3... | collective-permute-start | bytes 393224 | tf_op jit(solution)/shard_map/ppermute | solution.py:192
  47.8 6.5 %collective-permute-start.47 = (bf16[128,512]{1,0:T(8,128)(2,1)S(1)}, bf16[128,512]{1,0:T(8,128)(2,1)S(1)}, u32[]{:S(2)}, u32[]{:S(2)}) collective-permute-start(bf16[128,512]{1,0:T(8,128)(2,1)S(1)} %shard_map.92.x0), channel_id=1, source_target_pairs={{0,2},{1,3},{2,0},{3,1},{16,18},{17,19},{18,16},{19,17},{32,34},{3... | collective-permute-start | bytes 393224 | tf_op jit(solution)/shard_map/ppermute | solution.py:192
  48.1 9.4 %collective-permute-start.45 = (bf16[128,512]{1,0:T(8,128)(2,1)S(1)}, bf16[128,512]{1,0:T(8,128)(2,1)S(1)}, u32[]{:S(2)}, u32[]{:S(2)}) collective-permute-start(bf16[128,512]{1,0:T(8,128)(2,1)S(1)} %shard_map.92.x0), channel_id=1, source_target_pairs={{0,1},{1,2},{2,3},{3,0},{16,17},{17,18},{18,19},{19,16},{32,33},{3... | collective-permute-start | bytes 393224 | tf_op jit(solution)/shard_map/ppermute | solution.py:192
  58.7 6.8 %collective-permute-start.10 = (bf16[2,512,128]{2,1,0:T(8,128)(2,1)S(1)}, bf16[2,512,128]{2,1,0:T(8,128)(2,1)S(1)}, u32[]{:S(2)}, u32[]{:S(2)}) collective-permute-start(bf16[2,512,128]{2,1,0:T(8,128)(2,1)S(1)} %collective-permute-done.9.x), channel_id=1, source_target_pairs={{0,4},{4,0},{8,12},{12,8},{16,20},{20,16},{24,28},{28,24},{32,36},... | collective-permute-start | bytes 786440 | tf_op jit(solution)/shard_map/ppermute | solution.py:177
  59.9 16.8 %collective-permute-start.49 = (bf16[2,128,512]{2,1,0:T(8,128)(2,1)S(1)}, bf16[2,128,512]{2,1,0:T(8,128)(2,1)S(1)}, u32[]{:S(2)}, u32[]{:S(2)}) collective-permute-start(bf16[2,128,512]{2,1,0:T(8,128)(2,1)S(1)} %shard_map.96), channel_id=1, source_target_pairs={{0,112},{4,124},{8,120},{12,116},{16,0},{20,12},{24,8},{28,4},{32,... | collective-permute-start | bytes 786440 | tf_op jit(solution)/shard_map/ppermute | solution.py:184
  67.3 8.3 %collective-permute-start.11 = (bf16[512,128]{1,0:T(8,128)(2,1)S(1)}, bf16[512,128]{1,0:T(8,128)(2,1)S(1)}, u32[]{:S(2)}, u32[]{:S(2)}) collective-permute-start(bf16[512,128]{1,0:T(8,128)(2,1)S(1)} %get-tuple-element.46), channel_id=1, source_target_pairs={{0,1},{1,2},{2,3},{3,0},{16,17},{17,18},{18,19},{19,16},{32,33},{3... | collective-permute-start | bytes 393224 | tf_op jit(solution)/shard_map/ppermute | solution.py:192
  67.4 8.3 %collective-permute-start.12 = (bf16[512,128]{1,0:T(8,128)(2,1)S(1)}, bf16[512,128]{1,0:T(8,128)(2,1)S(1)}, u32[]{:S(2)}, u32[]{:S(2)}) collective-permute-start(bf16[512,128]{1,0:T(8,128)(2,1)S(1)} %get-tuple-element.45), channel_id=1, source_target_pairs={{0,2},{1,3},{2,0},{3,1},{16,18},{17,19},{18,16},{19,17},{32,34},{3... | collective-permute-start | bytes 393224 | tf_op jit(solution)/shard_map/ppermute | solution.py:192
  69.0 7.5 %collective-permute-start.13 = (bf16[512,128]{1,0:T(8,128)(2,1)S(1)}, bf16[512,128]{1,0:T(8,128)(2,1)S(1)}, u32[]{:S(2)}, u32[]{:S(2)}) collective-permute-start(bf16[512,128]{1,0:T(8,128)(2,1)S(1)} %get-tuple-element.44), channel_id=1, source_target_pairs={{0,3},{1,0},{2,1},{3,2},{16,19},{17,16},{18,17},{19,18},{32,35},{3... | collective-permute-start | bytes 393224 | tf_op jit(solution)/shard_map/ppermute | solution.py:192
  78.1 13.4 %collective-permute-start.15 = (bf16[2,512,128]{2,1,0:T(8,128)(2,1)S(1)}, bf16[2,512,128]{2,1,0:T(8,128)(2,1)S(1)}, u32[]{:S(2)}, u32[]{:S(2)}) collective-permute-start(bf16[2,512,128]{2,1,0:T(8,128)(2,1)S(1)} %shard_map.70), channel_id=1, source_target_pairs={{112,0},{116,12},{120,8},{124,4},{0,16},{4,28},{8,24},{12,20},{16,... | collective-permute-start | bytes 786440 | tf_op jit(solution)/shard_map/ppermute | solution.py:184
  78.5 5.6 %collective-permute-start.52 = (bf16[128,512]{1,0:T(8,128)(2,1)S(1)}, bf16[128,512]{1,0:T(8,128)(2,1)S(1)}, u32[]{:S(2)}, u32[]{:S(2)}) collective-permute-start(bf16[128,512]{1,0:T(8,128)(2,1)S(1)} %shard_map.97.x0), channel_id=1, source_target_pairs={{0,3},{1,0},{2,1},{3,2},{16,19},{17,16},{18,17},{19,18},{32,35},{3... | collective-permute-start | bytes 393224 | tf_op jit(solution)/shard_map/ppermute | solution.py:192
  80.8 6.1 %collective-permute-start.53 = (bf16[128,512]{1,0:T(8,128)(2,1)S(1)}, bf16[128,512]{1,0:T(8,128)(2,1)S(1)}, u32[]{:S(2)}, u32[]{:S(2)}) collective-permute-start(bf16[128,512]{1,0:T(8,128)(2,1)S(1)} %shard_map.97.x0), channel_id=1, source_target_pairs={{0,2},{1,3},{2,0},{3,1},{16,18},{17,19},{18,16},{19,17},{32,34},{3... | collective-permute-start | bytes 393224 | tf_op jit(solution)/shard_map/ppermute | solution.py:192
  80.9 9.1 %collective-permute-start.51 = (bf16[128,512]{1,0:T(8,128)(2,1)S(1)}, bf16[128,512]{1,0:T(8,128)(2,1)S(1)}, u32[]{:S(2)}, u32[]{:S(2)}) collective-permute-start(bf16[128,512]{1,0:T(8,128)(2,1)S(1)} %shard_map.97.x0), channel_id=1, source_target_pairs={{0,1},{1,2},{2,3},{3,0},{16,17},{17,18},{18,19},{19,16},{32,33},{3... | collective-permute-start | bytes 393224 | tf_op jit(solution)/shard_map/ppermute | solution.py:192
  90.6 3.8 %collective-permute-start.54 = (bf16[2,128,512]{2,1,0:T(8,128)(2,1)S(1)}, bf16[2,128,512]{2,1,0:T(8,128)(2,1)S(1)}, u32[]{:S(2)}, u32[]{:S(2)}) collective-permute-start(bf16[2,128,512]{2,1,0:T(8,128)(2,1)S(1)} %get-tuple-element.25), channel_id=1, source_target_pairs={{0,4},{4,0},{8,12},{12,8},{16,20},{20,16},{24,28},{28,24},{32,36},... | collective-permute-start | bytes 786440 | tf_op jit(solution)/shard_map/ppermute | solution.py:177
  91.5 7.0 %collective-permute-start.16 = (bf16[2,512,128]{2,1,0:T(8,128)(2,1)S(1)}, bf16[2,512,128]{2,1,0:T(8,128)(2,1)S(1)}, u32[]{:S(2)}, u32[]{:S(2)}) collective-permute-start(bf16[2,512,128]{2,1,0:T(8,128)(2,1)S(1)} %collective-permute-done.15.x), channel_id=1, source_target_pairs={{0,4},{4,0},{8,12},{12,8},{16,20},{20,16},{24,28},{28,24},{32,36},... | collective-permute-start | bytes 786440 | tf_op jit(solution)/shard_map/ppermute | solution.py:177
  92.3 10.8 %collective-permute-start.20 = (bf16[3,512,128]{2,1,0:T(8,128)(2,1)S(1)}, bf16[3,512,128]{2,1,0:T(8,128)(2,1)S(1)}, u32[]{:S(2)}, u32[]{:S(2)}) collective-permute-start(bf16[3,512,128]{2,1,0:T(8,128)(2,1)S(1)} %shard_map.73), channel_id=1, source_target_pairs={{0,112},{4,116},{8,120},{12,124},{16,0},{20,4},{24,8},{28,12},{32,... | collective-permute-start | bytes 1179656 | tf_op jit(solution)/shard_map/ppermute | solution.py:208
  94.5 15.1 %collective-permute-start.55 = (bf16[2,128,512]{2,1,0:T(8,128)(2,1)S(1)}, bf16[2,128,512]{2,1,0:T(8,128)(2,1)S(1)}, u32[]{:S(2)}, u32[]{:S(2)}) collective-permute-start(bf16[2,128,512]{2,1,0:T(8,128)(2,1)S(1)} %shard_map.101), channel_id=1, source_target_pairs={{0,112},{4,124},{8,120},{12,116},{16,0},{20,12},{24,8},{28,4},{32,... | collective-permute-start | bytes 786440 | tf_op jit(solution)/shard_map/ppermute | solution.py:184
  100.3 8.2 %collective-permute-start.17 = (bf16[512,128]{1,0:T(8,128)(2,1)S(1)}, bf16[512,128]{1,0:T(8,128)(2,1)S(1)}, u32[]{:S(2)}, u32[]{:S(2)}) collective-permute-start(bf16[512,128]{1,0:T(8,128)(2,1)S(1)} %get-tuple-element.43), channel_id=1, source_target_pairs={{0,1},{1,2},{2,3},{3,0},{16,17},{17,18},{18,19},{19,16},{32,33},{3... | collective-permute-start | bytes 393224 | tf_op jit(solution)/shard_map/ppermute | solution.py:192
  100.4 8.2 %collective-permute-start.18 = (bf16[512,128]{1,0:T(8,128)(2,1)S(1)}, bf16[512,128]{1,0:T(8,128)(2,1)S(1)}, u32[]{:S(2)}, u32[]{:S(2)}) collective-permute-start(bf16[512,128]{1,0:T(8,128)(2,1)S(1)} %get-tuple-element.42), channel_id=1, source_target_pairs={{0,2},{1,3},{2,0},{3,1},{16,18},{17,19},{18,16},{19,17},{32,34},{3... | collective-permute-start | bytes 393224 | tf_op jit(solution)/shard_map/ppermute | solution.py:192
  101.7 7.7 %collective-permute-start.19 = (bf16[512,128]{1,0:T(8,128)(2,1)S(1)}, bf16[512,128]{1,0:T(8,128)(2,1)S(1)}, u32[]{:S(2)}, u32[]{:S(2)}) collective-permute-start(bf16[512,128]{1,0:T(8,128)(2,1)S(1)} %get-tuple-element.41), channel_id=1, source_target_pairs={{0,3},{1,0},{2,1},{3,2},{16,19},{17,16},{18,17},{19,18},{32,35},{3... | collective-permute-start | bytes 393224 | tf_op jit(solution)/shard_map/ppermute | solution.py:192
  109.7 2.8 %collective-permute-start.56 = (bf16[128,512]{1,0:T(8,128)(2,1)S(1)}, bf16[128,512]{1,0:T(8,128)(2,1)S(1)}, u32[]{:S(2)}, u32[]{:S(2)}) collective-permute-start(bf16[128,512]{1,0:T(8,128)(2,1)S(1)} %slice_bitcast_fusion.3), channel_id=1, source_target_pairs={{0,4},{4,0},{8,12},{12,8},{16,20},{20,16},{24,28},{28,24},{32,36},... | collective-permute-start | bytes 393224 | tf_op jit(solution)/shard_map/ppermute | solution.py:177
  111.0 14.2 %collective-permute-start.22 = (bf16[2,512,128]{2,1,0:T(8,128)(2,1)S(1)}, bf16[2,512,128]{2,1,0:T(8,128)(2,1)S(1)}, u32[]{:S(2)}, u32[]{:S(2)}) collective-permute-start(bf16[2,512,128]{2,1,0:T(8,128)(2,1)S(1)} %shard_map.75), channel_id=1, source_target_pairs={{112,0},{116,12},{120,8},{124,4},{0,16},{4,28},{8,24},{12,20},{16,... | collective-permute-start | bytes 786440 | tf_op jit(solution)/shard_map/ppermute | solution.py:184
  112.5 5.1 %collective-permute-start.58 = (bf16[128,512]{1,0:T(8,128)(2,1)S(1)}, bf16[128,512]{1,0:T(8,128)(2,1)S(1)}, u32[]{:S(2)}, u32[]{:S(2)}) collective-permute-start(bf16[128,512]{1,0:T(8,128)(2,1)S(1)} %shard_map.102.x0), channel_id=1, source_target_pairs={{0,3},{1,0},{2,1},{3,2},{16,19},{17,16},{18,17},{19,18},{32,35},{3... | collective-permute-start | bytes 393224 | tf_op jit(solution)/shard_map/ppermute | solution.py:192
  114.6 5.7 %collective-permute-start.59 = (bf16[128,512]{1,0:T(8,128)(2,1)S(1)}, bf16[128,512]{1,0:T(8,128)(2,1)S(1)}, u32[]{:S(2)}, u32[]{:S(2)}) collective-permute-start(bf16[128,512]{1,0:T(8,128)(2,1)S(1)} %shard_map.102.x0), channel_id=1, source_target_pairs={{0,2},{1,3},{2,0},{3,1},{16,18},{17,19},{18,16},{19,17},{32,34},{3... | collective-permute-start | bytes 393224 | tf_op jit(solution)/shard_map/ppermute | solution.py:192
  114.6 9.1 %collective-permute-start.57 = (bf16[128,512]{1,0:T(8,128)(2,1)S(1)}, bf16[128,512]{1,0:T(8,128)(2,1)S(1)}, u32[]{:S(2)}, u32[]{:S(2)}) collective-permute-start(bf16[128,512]{1,0:T(8,128)(2,1)S(1)} %shard_map.102.x0), channel_id=1, source_target_pairs={{0,1},{1,2},{2,3},{3,0},{16,17},{17,18},{18,19},{19,16},{32,33},{3... | collective-permute-start | bytes 393224 | tf_op jit(solution)/shard_map/ppermute | solution.py:192
  125.2 6.4 %collective-permute-start.23 = (bf16[2,512,128]{2,1,0:T(8,128)(2,1)S(1)}, bf16[2,512,128]{2,1,0:T(8,128)(2,1)S(1)}, u32[]{:S(2)}, u32[]{:S(2)}) collective-permute-start(bf16[2,512,128]{2,1,0:T(8,128)(2,1)S(1)} %collective-permute-done.22.x), channel_id=1, source_target_pairs={{0,4},{4,0},{8,12},{12,8},{16,20},{20,16},{24,28},{28,24},{32,36},... | collective-permute-start | bytes 786440 | tf_op jit(solution)/shard_map/ppermute | solution.py:177
  126.4 17.8 %collective-permute-start.61 = (bf16[2,128,512]{2,1,0:T(8,128)(2,1)S(1)}, bf16[2,128,512]{2,1,0:T(8,128)(2,1)S(1)}, u32[]{:S(2)}, u32[]{:S(2)}) collective-permute-start(bf16[2,128,512]{2,1,0:T(8,128)(2,1)S(1)} %shard_map.106), channel_id=1, source_target_pairs={{0,112},{4,124},{8,120},{12,116},{16,0},{20,12},{24,8},{28,4},{32,... | collective-permute-start | bytes 786440 | tf_op jit(solution)/shard_map/ppermute | solution.py:184
  133.4 9.4 %collective-permute-start.24 = (bf16[512,128]{1,0:T(8,128)(2,1)S(1)}, bf16[512,128]{1,0:T(8,128)(2,1)S(1)}, u32[]{:S(2)}, u32[]{:S(2)}) collective-permute-start(bf16[512,128]{1,0:T(8,128)(2,1)S(1)} %get-tuple-element.40), channel_id=1, source_target_pairs={{0,1},{1,2},{2,3},{3,0},{16,17},{17,18},{18,19},{19,16},{32,33},{3... | collective-permute-start | bytes 393224 | tf_op jit(solution)/shard_map/ppermute | solution.py:192
  133.5 9.3 %collective-permute-start.25 = (bf16[512,128]{1,0:T(8,128)(2,1)S(1)}, bf16[512,128]{1,0:T(8,128)(2,1)S(1)}, u32[]{:S(2)}, u32[]{:S(2)}) collective-permute-start(bf16[512,128]{1,0:T(8,128)(2,1)S(1)} %get-tuple-element.39), channel_id=1, source_target_pairs={{0,2},{1,3},{2,0},{3,1},{16,18},{17,19},{18,16},{19,17},{32,34},{3... | collective-permute-start | bytes 393224 | tf_op jit(solution)/shard_map/ppermute | solution.py:192
  135.6 7.9 %collective-permute-start.26 = (bf16[512,128]{1,0:T(8,128)(2,1)S(1)}, bf16[512,128]{1,0:T(8,128)(2,1)S(1)}, u32[]{:S(2)}, u32[]{:S(2)}) collective-permute-start(bf16[512,128]{1,0:T(8,128)(2,1)S(1)} %get-tuple-element.38), channel_id=1, source_target_pairs={{0,3},{1,0},{2,1},{3,2},{16,19},{17,16},{18,17},{19,18},{32,35},{3... | collective-permute-start | bytes 393224 | tf_op jit(solution)/shard_map/ppermute | solution.py:192
  145.3 13.5 %collective-permute-start.28 = (bf16[2,512,128]{2,1,0:T(8,128)(2,1)S(1)}, bf16[2,512,128]{2,1,0:T(8,128)(2,1)S(1)}, u32[]{:S(2)}, u32[]{:S(2)}) collective-permute-start(bf16[2,512,128]{2,1,0:T(8,128)(2,1)S(1)} %shard_map.79), channel_id=1, source_target_pairs={{112,0},{116,12},{120,8},{124,4},{0,16},{4,28},{8,24},{12,20},{16,... | collective-permute-start | bytes 786440 | tf_op jit(solution)/shard_map/ppermute | solution.py:184
  145.8 5.4 %collective-permute-start.64 = (bf16[128,512]{1,0:T(8,128)(2,1)S(1)}, bf16[128,512]{1,0:T(8,128)(2,1)S(1)}, u32[]{:S(2)}, u32[]{:S(2)}) collective-permute-start(bf16[128,512]{1,0:T(8,128)(2,1)S(1)} %shard_map.107.x0), channel_id=1, source_target_pairs={{0,3},{1,0},{2,1},{3,2},{16,19},{17,16},{18,17},{19,18},{32,35},{3... | collective-permute-start | bytes 393224 | tf_op jit(solution)/shard_map/ppermute | solution.py:192
  148.1 6.2 %collective-permute-start.65 = (bf16[128,512]{1,0:T(8,128)(2,1)S(1)}, bf16[128,512]{1,0:T(8,128)(2,1)S(1)}, u32[]{:S(2)}, u32[]{:S(2)}) collective-permute-start(bf16[128,512]{1,0:T(8,128)(2,1)S(1)} %shard_map.107.x0), channel_id=1, source_target_pairs={{0,2},{1,3},{2,0},{3,1},{16,18},{17,19},{18,16},{19,17},{32,34},{3... | collective-permute-start | bytes 393224 | tf_op jit(solution)/shard_map/ppermute | solution.py:192
  148.1 9.1 %collective-permute-start.63 = (bf16[128,512]{1,0:T(8,128)(2,1)S(1)}, bf16[128,512]{1,0:T(8,128)(2,1)S(1)}, u32[]{:S(2)}, u32[]{:S(2)}) collective-permute-start(bf16[128,512]{1,0:T(8,128)(2,1)S(1)} %shard_map.107.x0), channel_id=1, source_target_pairs={{0,1},{1,2},{2,3},{3,0},{16,17},{17,18},{18,19},{19,16},{32,33},{3... | collective-permute-start | bytes 393224 | tf_op jit(solution)/shard_map/ppermute | solution.py:192
  157.9 2.0 collective-permute-start.66
  158.8 6.4 %collective-permute-start.29 = (bf16[2,512,128]{2,1,0:T(8,128)(2,1)S(1)}, bf16[2,512,128]{2,1,0:T(8,128)(2,1)S(1)}, u32[]{:S(2)}, u32[]{:S(2)}) collective-permute-start(bf16[2,512,128]{2,1,0:T(8,128)(2,1)S(1)} %collective-permute-done.28.x), channel_id=1, source_target_pairs={{0,4},{4,0},{8,12},{12,8},{16,20},{20,16},{24,28},{28,24},{32,36},... | collective-permute-start | bytes 786440 | tf_op jit(solution)/shard_map/ppermute | solution.py:177
  160.0 17.2 %collective-permute-start.67 = (bf16[2,128,512]{2,1,0:T(8,128)(2,1)S(1)}, bf16[2,128,512]{2,1,0:T(8,128)(2,1)S(1)}, u32[]{:S(2)}, u32[]{:S(2)}) collective-permute-start(bf16[2,128,512]{2,1,0:T(8,128)(2,1)S(1)} %shard_map.111), channel_id=1, source_target_pairs={{0,112},{4,124},{8,120},{12,116},{16,0},{20,12},{24,8},{28,4},{32,... | collective-permute-start | bytes 786440 | tf_op jit(solution)/shard_map/ppermute | solution.py:184
  166.9 8.7 %collective-permute-start.30 = (bf16[512,128]{1,0:T(8,128)(2,1)S(1)}, bf16[512,128]{1,0:T(8,128)(2,1)S(1)}, u32[]{:S(2)}, u32[]{:S(2)}) collective-permute-start(bf16[512,128]{1,0:T(8,128)(2,1)S(1)} %get-tuple-element.37), channel_id=1, source_target_pairs={{0,1},{1,2},{2,3},{3,0},{16,17},{17,18},{18,19},{19,16},{32,33},{3... | collective-permute-start | bytes 393224 | tf_op jit(solution)/shard_map/ppermute | solution.py:192
  167.0 8.7 %collective-permute-start.31 = (bf16[512,128]{1,0:T(8,128)(2,1)S(1)}, bf16[512,128]{1,0:T(8,128)(2,1)S(1)}, u32[]{:S(2)}, u32[]{:S(2)}) collective-permute-start(bf16[512,128]{1,0:T(8,128)(2,1)S(1)} %get-tuple-element.36), channel_id=1, source_target_pairs={{0,2},{1,3},{2,0},{3,1},{16,18},{17,19},{18,16},{19,17},{32,34},{3... | collective-permute-start | bytes 393224 | tf_op jit(solution)/shard_map/ppermute | solution.py:192
  168.8 7.8 %collective-permute-start.32 = (bf16[512,128]{1,0:T(8,128)(2,1)S(1)}, bf16[512,128]{1,0:T(8,128)(2,1)S(1)}, u32[]{:S(2)}, u32[]{:S(2)}) collective-permute-start(bf16[512,128]{1,0:T(8,128)(2,1)S(1)} %get-tuple-element.35), channel_id=1, source_target_pairs={{0,3},{1,0},{2,1},{3,2},{16,19},{17,16},{18,17},{19,18},{32,35},{3... | collective-permute-start | bytes 393224 | tf_op jit(solution)/shard_map/ppermute | solution.py:192
  178.2 13.5 %collective-permute-start.34 = (bf16[2,512,128]{2,1,0:T(8,128)(2,1)S(1)}, bf16[2,512,128]{2,1,0:T(8,128)(2,1)S(1)}, u32[]{:S(2)}, u32[]{:S(2)}) collective-permute-start(bf16[2,512,128]{2,1,0:T(8,128)(2,1)S(1)} %shard_map.83), channel_id=1, source_target_pairs={{112,0},{116,12},{120,8},{124,4},{0,16},{4,28},{8,24},{12,20},{16,... | collective-permute-start | bytes 786440 | tf_op jit(solution)/shard_map/ppermute | solution.py:184
  178.7 7.7 %collective-permute-start.70 = (bf16[128,512]{1,0:T(8,128)(2,1)S(1)}, bf16[128,512]{1,0:T(8,128)(2,1)S(1)}, u32[]{:S(2)}, u32[]{:S(2)}) collective-permute-start(bf16[128,512]{1,0:T(8,128)(2,1)S(1)} %shard_map.112.x0), channel_id=1, source_target_pairs={{0,3},{1,0},{2,1},{3,2},{16,19},{17,16},{18,17},{19,18},{32,35},{3... | collective-permute-start | bytes 393224 | tf_op jit(solution)/shard_map/ppermute | solution.py:192
  181.0 6.2 %collective-permute-start.71 = (bf16[128,512]{1,0:T(8,128)(2,1)S(1)}, bf16[128,512]{1,0:T(8,128)(2,1)S(1)}, u32[]{:S(2)}, u32[]{:S(2)}) collective-permute-start(bf16[128,512]{1,0:T(8,128)(2,1)S(1)} %shard_map.112.x0), channel_id=1, source_target_pairs={{0,2},{1,3},{2,0},{3,1},{16,18},{17,19},{18,16},{19,17},{32,34},{3... | collective-permute-start | bytes 393224 | tf_op jit(solution)/shard_map/ppermute | solution.py:192
  181.0 9.1 %collective-permute-start.69 = (bf16[128,512]{1,0:T(8,128)(2,1)S(1)}, bf16[128,512]{1,0:T(8,128)(2,1)S(1)}, u32[]{:S(2)}, u32[]{:S(2)}) collective-permute-start(bf16[128,512]{1,0:T(8,128)(2,1)S(1)} %shard_map.112.x0), channel_id=1, source_target_pairs={{0,1},{1,2},{2,3},{3,0},{16,17},{17,18},{18,19},{19,16},{32,33},{3... | collective-permute-start | bytes 393224 | tf_op jit(solution)/shard_map/ppermute | solution.py:192
  190.8 2.0 collective-permute-start.72
  191.7 5.0 %collective-permute-start.35 = (bf16[2,512,128]{2,1,0:T(8,128)(2,1)S(1)}, bf16[2,512,128]{2,1,0:T(8,128)(2,1)S(1)}, u32[]{:S(2)}, u32[]{:S(2)}) collective-permute-start(bf16[2,512,128]{2,1,0:T(8,128)(2,1)S(1)} %collective-permute-done.34.x), channel_id=1, source_target_pairs={{0,4},{4,0},{8,12},{12,8},{16,20},{20,16},{24,28},{28,24},{32,36},... | collective-permute-start | bytes 786440 | tf_op jit(solution)/shard_map/ppermute | solution.py:177
  192.9 8.6 %collective-permute-start.73 = (bf16[2,128,512]{2,1,0:T(8,128)(2,1)S(1)}, bf16[2,128,512]{2,1,0:T(8,128)(2,1)S(1)}, u32[]{:S(2)}, u32[]{:S(2)}) collective-permute-start(bf16[2,128,512]{2,1,0:T(8,128)(2,1)S(1)} %shard_map.116), channel_id=1, source_target_pairs={{0,0},{4,12},{8,8},{12,4},{16,16},{20,28},{24,24},{28,20},{32,32},... | collective-permute-start | bytes 786440 | tf_op jit(solution)/shard_map/ppermute | solution.py:188
  198.5 5.6 %collective-permute-start.36 = (bf16[512,128]{1,0:T(8,128)(2,1)S(1)}, bf16[512,128]{1,0:T(8,128)(2,1)S(1)}, u32[]{:S(2)}, u32[]{:S(2)}) collective-permute-start(bf16[512,128]{1,0:T(8,128)(2,1)S(1)} %get-tuple-element.34), channel_id=1, source_target_pairs={{0,1},{1,2},{2,3},{3,0},{16,17},{17,18},{18,19},{19,16},{32,33},{3... | collective-permute-start | bytes 393224 | tf_op jit(solution)/shard_map/ppermute | solution.py:192
  201.6 6.2 %collective-permute-start.37 = (bf16[512,128]{1,0:T(8,128)(2,1)S(1)}, bf16[512,128]{1,0:T(8,128)(2,1)S(1)}, u32[]{:S(2)}, u32[]{:S(2)}) collective-permute-start(bf16[512,128]{1,0:T(8,128)(2,1)S(1)} %get-tuple-element.33), channel_id=1, source_target_pairs={{0,2},{1,3},{2,0},{3,1},{16,18},{17,19},{18,16},{19,17},{32,34},{3... | collective-permute-start | bytes 393224 | tf_op jit(solution)/shard_map/ppermute | solution.py:192
  202.0 7.2 %collective-permute-start.38 = (bf16[512,128]{1,0:T(8,128)(2,1)S(1)}, bf16[512,128]{1,0:T(8,128)(2,1)S(1)}, u32[]{:S(2)}, u32[]{:S(2)}) collective-permute-start(bf16[512,128]{1,0:T(8,128)(2,1)S(1)} %get-tuple-element.32), channel_id=1, source_target_pairs={{0,3},{1,0},{2,1},{3,2},{16,19},{17,16},{18,17},{19,18},{32,35},{3... | collective-permute-start | bytes 393224 | tf_op jit(solution)/shard_map/ppermute | solution.py:192
  (16 other events, 51.3 us)
where the time goes:
time: 210 us
  waiting for transfers between devices  85.6 us (41%)
  starting transfers between devices  78.2 us (37%)
  Pallas kernels  42.8 us (20%)
    ppermute x36, waiting for transfers between devices, over_col(): return lax.ppermute(value, ('slab', 'col'), pairs)  72.6 us
    pallas_call x59, Pallas kernels, call(): pl.pallas_call(kernel, out_shape=outs, in_specs=specs or [VMEM] * len(arg...  42.8 us
    ppermute x36, starting transfers between devices, over_col(): return lax.ppermute(value, ('slab', 'col'), pairs)  33.6 us
    ppermute x10, starting transfers between devices, over_slab(): return lax.ppermute(value, ('slab', 'row'), pairs)  20.2 us
    ppermute x24, starting transfers between devices, swap_cores(): return lax.ppermute(value, ('slab', 'row'), pairs)  10.2 us
    ppermute x24, waiting for transfers between devices, swap_cores(): return lax.ppermute(value, ('slab', 'row'), pairs)  10 us
    ppermute x2, starting transfers between devices, over_half(): return lax.ppermute(value, ('slab', 'row'), pairs)  7.98 us
  transfers between devices with their start and end apart: 75, of which 43 were waited for; matrix products, arithmetic and copies ran while one was open for 0% of the time, Pallas kernels for 20%

commit v1 on v0

--- a/solution.py
+++ b/solution.py
@@ -67,30 +67,49 @@
     lax.fori_loop(0, count, step, 0)
 
 
-def first_kernel(plan, stored, up, down, after):
+def turn_kernel(blocks, out):
+    def step(i, carry):
+        out[i // 4, i % 4] = blocks[i // 4, i % 4].T
+        return carry
+
+    lax.fori_loop(0, 16, step, 0)
+
+
+def turned(value):
+    return narrow(wide(value).T)
+
+
+def first_kernel(plan, stored, up, down):
     slab = lax.axis_index("slab")
-    up[...] = stored[plan[0, 0, slab]]
-    down[...] = narrow(wide(stored[plan[0, 1, slab]]).T)
-    after[0] = stored[plan[1, 0, slab]]
-    after[1] = stored[plan[2, 0, slab]]
-
-
-def spread_kernel(gain, out):
-    row_gain = jnp.where(lax.axis_index("slab") == 7, 0.0, gain[...])
-    out[...] = jnp.broadcast_to(row_gain, (out.shape[1], out.shape[0])).T
+    down[...] = turned(stored[plan[0, 1, slab]])
+    up[...] = turned(stored[plan[0, 0, slab]])
 
 
 def pick_up_kernel(plan, stored, out):
     slab = lax.axis_index("slab")
-    for t in range(3, TICKS):
-        out[t - 3] = stored[plan[t, 0, slab]]
+
+    def step(t, carry):
+        out[t] = turned(stored[plan[t + 3, 0, slab]])
+        return carry
+
+    lax.fori_loop(0, TICKS - 3, step, 0)
+
+
+def pick_near_kernel(plan, stored, out):
+    slab = lax.axis_index("slab")
+
+    def step(t, carry):
+        out[t] = turned(stored[plan[t + 1, 0, slab]])
+        return carry
+
+    lax.fori_loop(0, 2, step, 0)
 
 
 def pick_down_kernel(plan, stored, out):
     slab = lax.axis_index("slab")
 
     def step(t, carry):
-        out[t] = narrow(wide(stored[plan[t + 1, 1, slab]]).T)
+        out[t] = turned(stored[plan[t + 1, 1, slab]])
         return carry
 
     lax.fori_loop(0, TICKS - 1, step, 0)
@@ -103,7 +122,7 @@
 
 def up_first_kernel(blocks, x, acc):
     def step(m, carry):
-        acc[m] = f32dot(blocks[m, 0], x[0]) + f32dot(blocks[m, 1], x[1])
+        acc[m] = f32dot(x[0], blocks[m, 0]) + f32dot(x[1], blocks[m, 1])
         return carry
 
     lax.fori_loop(0, 4, step, 0, unroll=2)
@@ -111,20 +130,21 @@
 
 def up_last_kernel(blocks, x, acc, out):
     def step(m, carry):
-        out[m] = narrow(acc[m] + f32dot(blocks[m, 2], x[0]) + f32dot(blocks[m, 3], x[1]))
-        return carry
-
-    lax.fori_loop(0, 4, step, 0)
+        out[m] = narrow(acc[m] + f32dot(x[0], blocks[m, 2]) + f32dot(x[1], blocks[m, 3]))
+        return carry
+
+    lax.fori_loop(0, 4, step, 0, unroll=True)
 
 
 def up_sum_kernel(own, p1, p2, p3, out):
-    out[...] = narrow(wide(own[0]) + wide(p1[...]) + wide(p2[...]) + wide(p3[...]))
+    out[...] = narrow((wide(own[0]) + wide(p1[...]) + wide(p2[...]) + wide(p3[...])).T)
 
 
 def up_next_kernel(t, own, p1, p2, p3, source, gain, out):
     carried = narrow(wide(own[0]) + wide(p1[...]) + wide(p2[...]) + wide(p3[...]))
     chosen = source[t if t < 2 else t - 2]
-    out[...] = narrow(wide(chosen) + gain[...] * wide(carried))
+    used = jnp.where(lax.axis_index("slab") == 7, 0.0, gain[...])
+    out[...] = narrow(wide(chosen) + used * wide(carried))
 
 
 def down_first_kernel(blocks, x0, acc):
@@ -149,7 +169,7 @@
         kept[j] = acc[j] + f32dot(x3[...], blocks[3, j])
         return carry
 
-    lax.fori_loop(0, 2, step, 0)
+    lax.fori_loop(0, 2, step, 0, unroll=True)
 
 
 def down_pair_kernel(kept, got, out):
@@ -196,15 +216,15 @@
     down_gain = coupling[0, 1][None, :]
     piece_u = shape(piece, width)
     piece_d = shape(width, piece)
-    pair_u = shape(2, piece, width)
     pair_d = shape(2, width, piece)
     kept_d = shape(2, width, piece, kind=jnp.float32)
-    acc_up = shape(cols, piece, width, kind=jnp.float32)
+    acc_up = shape(cols, width, piece, kind=jnp.float32)
     acc_down = shape(rows, width, piece, kind=jnp.float32)
-    up_in, down_in, after = call(first_kernel, (piece_u, piece_d, pair_u), plan, stored, specs=[SMEM, VMEM])
+    up_in, down_in = call(first_kernel, (piece_d, piece_d), plan, stored, specs=[SMEM, VMEM])
     shift_pairs = [(s * rows + r, ((s - 1) % slabs) * rows + r) for s in everyone for r in range(rows)]
-    next_source = lax.ppermute(after, ("slab", "row"), shift_pairs)
-    later = call(pick_up_kernel, shape(TICKS - 3, piece, width), plan, stored, specs=[SMEM, VMEM])
+    near = call(pick_near_kernel, pair_d, plan, stored, specs=[SMEM, VMEM])
+    next_source = lax.ppermute(near, ("slab", "row"), shift_pairs)
+    later = call(pick_up_kernel, shape(TICKS - 3, width, piece), plan, stored, specs=[SMEM, VMEM])
     later = lax.ppermute(later, ("slab", "row"), shift_pairs)
     next_gain = lax.ppermute(coupling[0, 0], ("slab", "row"), shift_pairs)[None, :]
     blocks = call(
@@ -215,7 +235,7 @@
         scratch=[pltpu.VMEM((8, 256, rows, piece), jnp.bfloat16), pltpu.SemaphoreType.DMA((8,))],
         limit=40 << 20,
     )
-    up_gain = call(spread_kernel, shape(piece, width, kind=jnp.float32), next_gain)
+    columns = call(turn_kernel, shape(cols, rows, piece, piece), blocks, limit=20 << 20)
     down_sources = call(pick_down_kernel, shape(TICKS - 1, width, piece), plan, stored, specs=[SMEM, VMEM])
     for t in range(TICKS):
         last = t == TICKS - 1
@@ -228,7 +248,7 @@
         d3 = over_col(down_in, down_on, -3)
         other = swap_cores(up_in, senders)
         acc_d = call(down_first_kernel, acc_down, blocks, down_in)
-        pair = call(stack_kernel, pair_u, up_in, other)
+        pair = call(stack_kernel, pair_d, up_in, other)
         if t == 0:
             moved = over_half(pair, up_on)
         else:
@@ -237,13 +257,13 @@
         kept, sent = call(down_last_kernel, (kept_d, pair_d), blocks, d3, acc_d)
         got = swap_cores(sent, down_on)
         other = swap_cores(moved, up_on)
-        acc_u = call(up_first_kernel, acc_up, blocks, moved)
+        acc_u = call(up_first_kernel, acc_up, columns, moved)
         pair = call(down_pair_kernel, pair_d, kept, got)
         if last:
             moved_d = over_half(pair, down_on)
         else:
             moved_d = over_slab(pair, down_on, -1)
-        made = call(up_last_kernel, shape(cols, piece, width), blocks, other, acc_u)
+        made = call(up_last_kernel, shape(cols, width, piece), columns, other, acc_u)
         parts = [made] + [over_col(made[m], up_on, m) for m in (1, 2, 3)]
         got = swap_cores(moved_d[1], down_on)
         if last:
@@ -255,13 +275,13 @@
             )
             up_in = call(
                 lambda *refs, t=t: up_next_kernel(t, *refs),
-                piece_u,
+                piece_d,
                 parts[0],
                 parts[1],
                 parts[2],
                 parts[3],
                 later if t > 1 else next_source,
-                up_gain,
+                next_gain,
             )
     return (up_out[None], down_out[None])
 

time: 210 us -> 227 us (1.081)
  the two profiles are of different devices: /device:TPU:1 before, /device:TPU:16 now
where the time goes in v1:
time: 227 us; the launch traced here: 223 us
  starting transfers between devices  106 us (47%)
  waiting for transfers between devices  76.9 us (34%)
  Pallas kernels  36.6 us (16%)
    ppermute x36, starting transfers between devices, over_col(): return lax.ppermute(value, ('slab', 'col'), pairs)  57.3 us
    ppermute x36, waiting for transfers between devices, over_col(): return lax.ppermute(value, ('slab', 'col'), pairs)  38.1 us
    pallas_call x60, Pallas kernels, call(): pl.pallas_call(kernel, out_shape=outs, in_specs=specs or [VMEM] * len(arg...  36.6 us
    ppermute x10, waiting for transfers between devices, over_slab(): return lax.ppermute(value, ('slab', 'row'), pairs)  30.9 us
    ppermute x10, starting transfers between devices, over_slab(): return lax.ppermute(value, ('slab', 'row'), pairs)  21.9 us
    ppermute x24, starting transfers between devices, swap_cores(): return lax.ppermute(value, ('slab', 'row'), pairs)  20.7 us
    ppermute x24, waiting for transfers between devices, swap_cores(): return lax.ppermute(value, ('slab', 'row'), pairs)  7.89 us
  transfers between devices with their start and end apart: 75, of which 35 were waited for; matrix products, arithmetic and copies ran while one was open for 0% of the time, Pallas kernels for 15%

profile of v1, /device:TPU:16, one launch (start us, length us, event | category | flops | bytes accessed | tf_op | source)
XLA Modules:
  0.0 222.8 jit_solution(3838889161486541074)
XLA Ops:
  0.6 1.0 copy-done
  3.2 2.8 %collective-permute-start.40 = (bf16[128,512]{1,0:T(8,128)(2,1)S(1)}, bf16[128,512]{1,0:T(8,128)(2,1)S(1)}, u32[]{:S(2)}, u32[]{:S(2)}) collective-permute-start(bf16[128,512]{1,0:T(8,128)(2,1)S(1)} %get-tuple-element.17.x0), channel_id=1, source_target_pairs={{0,3},{1,0},{2,1},{3,2},{16,19},{17,16},{18,17},{19,18},{32,35},{3... | collective-permute-start | bytes 393224 | tf_op jit(solution)/shard_map/ppermute | solution.py:212
  7.7 3.7 %shard_map.59.blocks = bf16[4,4,512,512]{3,2,1,0:T(8,128)(2,1)S(1)} custom-call(bf16[2048,4,512]{2,1,0:T(4,128)(2,1)} %bitcast.70), custom_call_target="tpu_custom_call" | custom-call | tf_op jit(solution)/shard_map/pallas_call | solution.py:33
  12.3 1.5 collective-permute-done.41.x2
  16.3 1.2 collective-permute-done.other
  18.3 1.9 collective-permute-start.43
  21.2 9.4 %collective-permute-start.2 = (bf16[2,128,512]{2,1,0:T(8,128)(2,1)S(1)}, bf16[2,128,512]{2,1,0:T(8,128)(2,1)S(1)}, u32[]{:S(2)}, u32[]{:S(2)}) collective-permute-start(bf16[2,128,512]{2,1,0:T(8,128)(2,1)S(1)} %collective-permute-done.1.x), channel_id=1, source_target_pairs={{0,4},{4,0},{8,12},{12,8},{16,20},{20,16},{24,28},{28,24},{32,36},... | collective-permute-start | bytes 786440 | tf_op jit(solution)/shard_map/ppermute | solution.py:197
  30.8 2.6 %collective-permute-start.7 = (f32[512]{0:T(512)S(1)}, f32[512]{0:T(512)S(1)}, u32[]{:S(2)}, u32[]{:S(2)}) collective-permute-start(f32[512]{0:T(512)S(1)} %bitcast.73), channel_id=1, source_target_pairs={{0,112},{4,116},{8,120},{12,124},{16,0},{20,4},{24,8},{28,12},{32,... | collective-permute-start | bytes 6152 | tf_op jit(solution)/shard_map/ppermute | solution.py:229
  33.3 1.2 shard_map.92.refs_2_
  34.5 3.1 %shard_map.60.blocks = bf16[4,4,512,512]{3,2,1,0:T(8,128)(2,1)S(1)} custom-call(bf16[4,4,512,512]{3,2,1,0:T(8,128)(2,1)S(1)} %shard_map.59.blocks), custom_call_target="tpu_custom_call" | custom-call | tf_op jit(solution)/shard_map/pallas_call | solution.py:33
  41.6 4.1 %collective-permute-done.46.x1 = bf16[128,512]{1,0:T(8,128)(2,1)S(1)} collective-permute-done((bf16[128,512]{1,0:T(8,128)(2,1)S(1)}, bf16[128,512]{1,0:T(8,128)(2,1)S(1)}, u32[]{:S(2)}, u32[]{:S(2)}) %collective-permute-start.46) | collective-permute-done | bytes 131104 | tf_op jit(solution)/shard_map/ppermute | solution.py:212
  45.8 2.4 %collective-permute-done.47.x2 = bf16[128,512]{1,0:T(8,128)(2,1)S(1)} collective-permute-done((bf16[128,512]{1,0:T(8,128)(2,1)S(1)}, bf16[128,512]{1,0:T(8,128)(2,1)S(1)}, u32[]{:S(2)}, u32[]{:S(2)}) %collective-permute-start.47) | collective-permute-done | bytes 131104 | tf_op jit(solution)/shard_map/ppermute | solution.py:212
  49.9 1.6 collective-permute-start.5
  54.0 1.2 collective-permute-done.4.refs_2_
  56.2 1.3 collective-permute-done.8.other
  58.3 2.3 %collective-permute-start.49 = (bf16[2,128,512]{2,1,0:T(8,128)(2,1)S(1)}, bf16[2,128,512]{2,1,0:T(8,128)(2,1)S(1)}, u32[]{:S(2)}, u32[]{:S(2)}) collective-permute-start(bf16[2,128,512]{2,1,0:T(8,128)(2,1)S(1)} %shard_map.97), channel_id=1, source_target_pairs={{0,112},{4,124},{8,120},{12,116},{16,0},{20,12},{24,8},{28,4},{32,... | collective-permute-start | bytes 786440 | tf_op jit(solution)/shard_map/ppermute | solution.py:204
  60.6 6.6 %collective-permute-done.9.x = bf16[2,128,512]{2,1,0:T(8,128)(2,1)S(1)} collective-permute-done((bf16[2,128,512]{2,1,0:T(8,128)(2,1)S(1)}, bf16[2,128,512]{2,1,0:T(8,128)(2,1)S(1)}, u32[]{:S(2)}, u32[]{:S(2)}) %collective-permute-start.9) | collective-permute-done | bytes 262176 | tf_op jit(solution)/shard_map/ppermute | solution.py:204
  70.3 2.9 %collective-permute-start.52 = (bf16[128,512]{1,0:T(8,128)(2,1)S(1)}, bf16[128,512]{1,0:T(8,128)(2,1)S(1)}, u32[]{:S(2)}, u32[]{:S(2)}) collective-permute-start(bf16[128,512]{1,0:T(8,128)(2,1)S(1)} %shard_map.98.x0), channel_id=1, source_target_pairs={{0,3},{1,0},{2,1},{3,2},{16,19},{17,16},{18,17},{19,18},{32,35},{3... | collective-permute-start | bytes 393224 | tf_op jit(solution)/shard_map/ppermute | solution.py:212
  74.2 2.6 %collective-permute-start.11 = (bf16[128,512]{1,0:T(8,128)(2,1)S(1)}, bf16[128,512]{1,0:T(8,128)(2,1)S(1)}, u32[]{:S(2)}, u32[]{:S(2)}) collective-permute-start(bf16[128,512]{1,0:T(8,128)(2,1)S(1)} %get-tuple-element.44), channel_id=1, source_target_pairs={{0,1},{1,2},{2,3},{3,0},{16,17},{17,18},{18,19},{19,16},{32,33},{3... | collective-permute-start | bytes 393224 | tf_op jit(solution)/shard_map/ppermute | solution.py:212
  76.8 1.2 collective-permute-start.12
  79.0 2.8 %collective-permute-done.52.x1 = bf16[128,512]{1,0:T(8,128)(2,1)S(1)} collective-permute-done((bf16[128,512]{1,0:T(8,128)(2,1)S(1)}, bf16[128,512]{1,0:T(8,128)(2,1)S(1)}, u32[]{:S(2)}, u32[]{:S(2)}) %collective-permute-start.52) | collective-permute-done | bytes 131104 | tf_op jit(solution)/shard_map/ppermute | solution.py:212
  81.7 3.8 %collective-permute-start.13 = (bf16[128,512]{1,0:T(8,128)(2,1)S(1)}, bf16[128,512]{1,0:T(8,128)(2,1)S(1)}, u32[]{:S(2)}, u32[]{:S(2)}) collective-permute-start(bf16[128,512]{1,0:T(8,128)(2,1)S(1)} %get-tuple-element.42), channel_id=1, source_target_pairs={{0,3},{1,0},{2,1},{3,2},{16,19},{17,16},{18,17},{19,18},{32,35},{3... | collective-permute-start | bytes 393224 | tf_op jit(solution)/shard_map/ppermute | solution.py:212
  86.9 1.4 collective-permute-done.12.refs_2_
  88.5 1.3 collective-permute-done.14.other
  89.9 2.8 %collective-permute-start.15 = (bf16[2,128,512]{2,1,0:T(8,128)(2,1)S(1)}, bf16[2,128,512]{2,1,0:T(8,128)(2,1)S(1)}, u32[]{:S(2)}, u32[]{:S(2)}) collective-permute-start(bf16[2,128,512]{2,1,0:T(8,128)(2,1)S(1)} %shard_map.71), channel_id=1, source_target_pairs={{112,0},{116,12},{120,8},{124,4},{0,16},{4,28},{8,24},{12,20},{16,... | collective-permute-start | bytes 786440 | tf_op jit(solution)/shard_map/ppermute | solution.py:204
  93.0 7.0 %collective-permute-done.15.x = bf16[2,128,512]{2,1,0:T(8,128)(2,1)S(1)} collective-permute-done((bf16[2,128,512]{2,1,0:T(8,128)(2,1)S(1)}, bf16[2,128,512]{2,1,0:T(8,128)(2,1)S(1)}, u32[]{:S(2)}, u32[]{:S(2)}) %collective-permute-start.15) | collective-permute-done | bytes 262176 | tf_op jit(solution)/shard_map/ppermute | solution.py:204
  100.0 1.0 collective-permute-done.55.refs_0_
  102.3 1.9 collective-permute-start.20
  105.9 3.4 %collective-permute-start.58 = (bf16[128,512]{1,0:T(8,128)(2,1)S(1)}, bf16[128,512]{1,0:T(8,128)(2,1)S(1)}, u32[]{:S(2)}, u32[]{:S(2)}) collective-permute-start(bf16[128,512]{1,0:T(8,128)(2,1)S(1)} %shard_map.103.x0), channel_id=1, source_target_pairs={{0,3},{1,0},{2,1},{3,2},{16,19},{17,16},{18,17},{19,18},{32,35},{3... | collective-permute-start | bytes 393224 | tf_op jit(solution)/shard_map/ppermute | solution.py:212
  110.2 2.6 %collective-permute-start.17 = (bf16[128,512]{1,0:T(8,128)(2,1)S(1)}, bf16[128,512]{1,0:T(8,128)(2,1)S(1)}, u32[]{:S(2)}, u32[]{:S(2)}) collective-permute-start(bf16[128,512]{1,0:T(8,128)(2,1)S(1)} %get-tuple-element.41), channel_id=1, source_target_pairs={{0,1},{1,2},{2,3},{3,0},{16,17},{17,18},{18,19},{19,16},{32,33},{3... | collective-permute-start | bytes 393224 | tf_op jit(solution)/shard_map/ppermute | solution.py:212
  113.7 1.4 collective-permute-done.58.x1
  115.2 1.9 collective-permute-done.59.x2
  117.1 1.8 collective-permute-start.19
  120.3 1.7 collective-permute-done.17.refs_1_
  122.0 2.5 %collective-permute-done.18.refs_2_ = bf16[128,512]{1,0:T(8,128)(2,1)S(1)} collective-permute-done((bf16[128,512]{1,0:T(8,128)(2,1)S(1)}, bf16[128,512]{1,0:T(8,128)(2,1)S(1)}, u32[]{:S(2)}, u32[]{:S(2)}) %collective-permute-start.18) | collective-permute-done | bytes 131104 | tf_op jit(solution)/shard_map/ppermute | solution.py:212
  125.7 1.3 collective-permute-done.21.other
  127.1 3.6 %collective-permute-start.22 = (bf16[2,128,512]{2,1,0:T(8,128)(2,1)S(1)}, bf16[2,128,512]{2,1,0:T(8,128)(2,1)S(1)}, u32[]{:S(2)}, u32[]{:S(2)}) collective-permute-start(bf16[2,128,512]{2,1,0:T(8,128)(2,1)S(1)} %shard_map.76), channel_id=1, source_target_pairs={{112,0},{116,12},{120,8},{124,4},{0,16},{4,28},{8,24},{12,20},{16,... | collective-permute-start | bytes 786440 | tf_op jit(solution)/shard_map/ppermute | solution.py:204
  130.8 5.5 %collective-permute-done.22.x = bf16[2,128,512]{2,1,0:T(8,128)(2,1)S(1)} collective-permute-done((bf16[2,128,512]{2,1,0:T(8,128)(2,1)S(1)}, bf16[2,128,512]{2,1,0:T(8,128)(2,1)S(1)}, u32[]{:S(2)}, u32[]{:S(2)}) %collective-permute-start.22) | collective-permute-done | bytes 262176 | tf_op jit(solution)/shard_map/ppermute | solution.py:204
  136.3 1.1 collective-permute-start.23
  137.4 1.5 collective-permute-done.61.refs_0_
  140.9 2.4 %collective-permute-start.64 = (bf16[128,512]{1,0:T(8,128)(2,1)S(1)}, bf16[128,512]{1,0:T(8,128)(2,1)S(1)}, u32[]{:S(2)}, u32[]{:S(2)}) collective-permute-start(bf16[128,512]{1,0:T(8,128)(2,1)S(1)} %shard_map.108.x0), channel_id=1, source_target_pairs={{0,3},{1,0},{2,1},{3,2},{16,19},{17,16},{18,17},{19,18},{32,35},{3... | collective-permute-start | bytes 393224 | tf_op jit(solution)/shard_map/ppermute | solution.py:212
  143.3 1.2 collective-permute-start.63
  144.5 2.4 %collective-permute-start.24 = (bf16[128,512]{1,0:T(8,128)(2,1)S(1)}, bf16[128,512]{1,0:T(8,128)(2,1)S(1)}, u32[]{:S(2)}, u32[]{:S(2)}) collective-permute-start(bf16[128,512]{1,0:T(8,128)(2,1)S(1)} %get-tuple-element.38), channel_id=1, source_target_pairs={{0,1},{1,2},{2,3},{3,0},{16,17},{17,18},{18,19},{19,16},{32,33},{3... | collective-permute-start | bytes 393224 | tf_op jit(solution)/shard_map/ppermute | solution.py:212
  146.9 1.2 collective-permute-start.25
  149.0 3.1 %collective-permute-done.64.x1 = bf16[128,512]{1,0:T(8,128)(2,1)S(1)} collective-permute-done((bf16[128,512]{1,0:T(8,128)(2,1)S(1)}, bf16[128,512]{1,0:T(8,128)(2,1)S(1)}, u32[]{:S(2)}, u32[]{:S(2)}) %collective-permute-start.64) | collective-permute-done | bytes 131104 | tf_op jit(solution)/shard_map/ppermute | solution.py:212
  152.1 3.7 %collective-permute-start.26 = (bf16[128,512]{1,0:T(8,128)(2,1)S(1)}, bf16[128,512]{1,0:T(8,128)(2,1)S(1)}, u32[]{:S(2)}, u32[]{:S(2)}) collective-permute-start(bf16[128,512]{1,0:T(8,128)(2,1)S(1)} %get-tuple-element.36), channel_id=1, source_target_pairs={{0,3},{1,0},{2,1},{3,2},{16,19},{17,16},{18,17},{19,18},{32,35},{3... | collective-permute-start | bytes 393224 | tf_op jit(solution)/shard_map/ppermute | solution.py:212
  157.3 1.4 collective-permute-done.25.refs_2_
  158.9 1.3 collective-permute-done.27.other
  160.2 4.5 %collective-permute-start.28 = (bf16[2,128,512]{2,1,0:T(8,128)(2,1)S(1)}, bf16[2,128,512]{2,1,0:T(8,128)(2,1)S(1)}, u32[]{:S(2)}, u32[]{:S(2)}) collective-permute-start(bf16[2,128,512]{2,1,0:T(8,128)(2,1)S(1)} %shard_map.80), channel_id=1, source_target_pairs={{112,0},{116,12},{120,8},{124,4},{0,16},{4,28},{8,24},{12,20},{16,... | collective-permute-start | bytes 786440 | tf_op jit(solution)/shard_map/ppermute | solution.py:204
  164.9 4.3 %collective-permute-done.28.x = bf16[2,128,512]{2,1,0:T(8,128)(2,1)S(1)} collective-permute-done((bf16[2,128,512]{2,1,0:T(8,128)(2,1)S(1)}, bf16[2,128,512]{2,1,0:T(8,128)(2,1)S(1)}, u32[]{:S(2)}, u32[]{:S(2)}) %collective-permute-start.28) | collective-permute-done | bytes 262176 | tf_op jit(solution)/shard_map/ppermute | solution.py:204
  169.3 1.3 collective-permute-start.29
  170.5 1.5 collective-permute-done.67.refs_0_
  174.7 3.6 %collective-permute-start.70 = (bf16[128,512]{1,0:T(8,128)(2,1)S(1)}, bf16[128,512]{1,0:T(8,128)(2,1)S(1)}, u32[]{:S(2)}, u32[]{:S(2)}) collective-permute-start(bf16[128,512]{1,0:T(8,128)(2,1)S(1)} %shard_map.113.x0), channel_id=1, source_target_pairs={{0,3},{1,0},{2,1},{3,2},{16,19},{17,16},{18,17},{19,18},{32,35},{3... | collective-permute-start | bytes 393224 | tf_op jit(solution)/shard_map/ppermute | solution.py:212
  179.2 2.6 %collective-permute-start.30 = (bf16[128,512]{1,0:T(8,128)(2,1)S(1)}, bf16[128,512]{1,0:T(8,128)(2,1)S(1)}, u32[]{:S(2)}, u32[]{:S(2)}) collective-permute-start(bf16[128,512]{1,0:T(8,128)(2,1)S(1)} %get-tuple-element.35), channel_id=1, source_target_pairs={{0,1},{1,2},{2,3},{3,0},{16,17},{17,18},{18,19},{19,16},{32,33},{3... | collective-permute-start | bytes 393224 | tf_op jit(solution)/shard_map/ppermute | solution.py:212
  181.8 1.2 collective-permute-start.31
  183.0 3.8 %collective-permute-done.70.x1 = bf16[128,512]{1,0:T(8,128)(2,1)S(1)} collective-permute-done((bf16[128,512]{1,0:T(8,128)(2,1)S(1)}, bf16[128,512]{1,0:T(8,128)(2,1)S(1)}, u32[]{:S(2)}, u32[]{:S(2)}) %collective-permute-start.70) | collective-permute-done | bytes 131104 | tf_op jit(solution)/shard_map/ppermute | solution.py:212
  186.8 3.7 %collective-permute-start.32 = (bf16[128,512]{1,0:T(8,128)(2,1)S(1)}, bf16[128,512]{1,0:T(8,128)(2,1)S(1)}, u32[]{:S(2)}, u32[]{:S(2)}) collective-permute-start(bf16[128,512]{1,0:T(8,128)(2,1)S(1)} %get-tuple-element.33), channel_id=1, source_target_pairs={{0,3},{1,0},{2,1},{3,2},{16,19},{17,16},{18,17},{19,18},{32,35},{3... | collective-permute-start | bytes 393224 | tf_op jit(solution)/shard_map/ppermute | solution.py:212
  193.6 1.3 collective-permute-done.33.other
  194.9 5.6 %collective-permute-start.34 = (bf16[2,128,512]{2,1,0:T(8,128)(2,1)S(1)}, bf16[2,128,512]{2,1,0:T(8,128)(2,1)S(1)}, u32[]{:S(2)}, u32[]{:S(2)}) collective-permute-start(bf16[2,128,512]{2,1,0:T(8,128)(2,1)S(1)} %shard_map.84), channel_id=1, source_target_pairs={{112,0},{116,12},{120,8},{124,4},{0,16},{4,28},{8,24},{12,20},{16,... | collective-permute-start | bytes 786440 | tf_op jit(solution)/shard_map/ppermute | solution.py:204
  201.2 3.1 %collective-permute-done.34.x = bf16[2,128,512]{2,1,0:T(8,128)(2,1)S(1)} collective-permute-done((bf16[2,128,512]{2,1,0:T(8,128)(2,1)S(1)}, bf16[2,128,512]{2,1,0:T(8,128)(2,1)S(1)}, u32[]{:S(2)}, u32[]{:S(2)}) %collective-permute-start.34) | collective-permute-done | bytes 262176 | tf_op jit(solution)/shard_map/ppermute | solution.py:204
  206.1 4.1 %collective-permute-start.74 = (bf16[128,512]{1,0:T(8,128)(2,1)S(1)}, bf16[128,512]{1,0:T(8,128)(2,1)S(1)}, u32[]{:S(2)}, u32[]{:S(2)}) collective-permute-start(bf16[128,512]{1,0:T(8,128)(2,1)S(1)} %slice_bitcast_fusion), channel_id=1, source_target_pairs={{0,4},{4,0},{8,12},{12,8},{16,20},{20,16},{24,28},{28,24},{32,36},... | collective-permute-start | bytes 393224 | tf_op jit(solution)/shard_map/ppermute | solution.py:197
  211.1 4.8 %collective-permute-start.37 = (bf16[128,512]{1,0:T(8,128)(2,1)S(1)}, bf16[128,512]{1,0:T(8,128)(2,1)S(1)}, u32[]{:S(2)}, u32[]{:S(2)}) collective-permute-start(bf16[128,512]{1,0:T(8,128)(2,1)S(1)} %get-tuple-element.31), channel_id=1, source_target_pairs={{0,2},{1,3},{2,0},{3,1},{16,18},{17,19},{18,16},{19,17},{32,34},{3... | collective-permute-start | bytes 393224 | tf_op jit(solution)/shard_map/ppermute | solution.py:212
  216.6 1.5 collective-permute-done.36.p1
  218.1 4.0 %collective-permute-done.37.p2 = bf16[128,512]{1,0:T(8,128)(2,1)S(1)} collective-permute-done((bf16[128,512]{1,0:T(8,128)(2,1)S(1)}, bf16[128,512]{1,0:T(8,128)(2,1)S(1)}, u32[]{:S(2)}, u32[]{:S(2)}) %collective-permute-start.37) | collective-permute-done | bytes 131104 | tf_op jit(solution)/shard_map/ppermute | solution.py:212
  (169 shorter events, 49.0 us)
Async XLA Ops:
  3.2 9.2 %collective-permute-start.40 = (bf16[128,512]{1,0:T(8,128)(2,1)S(1)}, bf16[128,512]{1,0:T(8,128)(2,1)S(1)}, u32[]{:S(2)}, u32[]{:S(2)}) collective-permute-start(bf16[128,512]{1,0:T(8,128)(2,1)S(1)} %get-tuple-element.17.x0), channel_id=1, source_target_pairs={{0,3},{1,0},{2,1},{3,2},{16,19},{17,16},{18,17},{19,18},{32,35},{3... | collective-permute-start | bytes 393224 | tf_op jit(solution)/shard_map/ppermute | solution.py:212
  6.0 7.9 %collective-permute-start.41 = (bf16[128,512]{1,0:T(8,128)(2,1)S(1)}, bf16[128,512]{1,0:T(8,128)(2,1)S(1)}, u32[]{:S(2)}, u32[]{:S(2)}) collective-permute-start(bf16[128,512]{1,0:T(8,128)(2,1)S(1)} %get-tuple-element.17.x0), channel_id=1, source_target_pairs={{0,2},{1,3},{2,0},{3,1},{16,18},{17,19},{18,16},{19,17},{32,34},{3... | collective-permute-start | bytes 393224 | tf_op jit(solution)/shard_map/ppermute | solution.py:212
  6.8 8.5 %collective-permute-start.39 = (bf16[128,512]{1,0:T(8,128)(2,1)S(1)}, bf16[128,512]{1,0:T(8,128)(2,1)S(1)}, u32[]{:S(2)}, u32[]{:S(2)}) collective-permute-start(bf16[128,512]{1,0:T(8,128)(2,1)S(1)} %get-tuple-element.17.x0), channel_id=1, source_target_pairs={{0,1},{1,2},{2,3},{3,0},{16,17},{17,18},{18,19},{19,16},{32,33},{3... | collective-permute-start | bytes 393224 | tf_op jit(solution)/shard_map/ppermute | solution.py:212
  17.5 3.7 %collective-permute-start.1 = (bf16[2,128,512]{2,1,0:T(8,128)(2,1)S(1)}, bf16[2,128,512]{2,1,0:T(8,128)(2,1)S(1)}, u32[]{:S(2)}, u32[]{:S(2)}) collective-permute-start(bf16[2,128,512]{2,1,0:T(8,128)(2,1)S(1)} %shard_map.62), channel_id=1, source_target_pairs={{0,0},{4,12},{8,8},{12,4},{16,16},{20,28},{24,24},{28,20},{32,32},... | collective-permute-start | bytes 786440 | tf_op jit(solution)/shard_map/ppermute | solution.py:208
  18.3 12.3 %collective-permute-start.43 = (bf16[2,128,512]{2,1,0:T(8,128)(2,1)S(1)}, bf16[2,128,512]{2,1,0:T(8,128)(2,1)S(1)}, u32[]{:S(2)}, u32[]{:S(2)}) collective-permute-start(bf16[2,128,512]{2,1,0:T(8,128)(2,1)S(1)} %shard_map.91), channel_id=1, source_target_pairs={{0,112},{4,124},{8,120},{12,116},{16,0},{20,12},{24,8},{28,4},{32,... | collective-permute-start | bytes 786440 | tf_op jit(solution)/shard_map/ppermute | solution.py:204
  21.0 32.9 %collective-permute-start.6 = (bf16[2,128,512]{2,1,0:T(8,128)(2,1)S(1)}, bf16[2,128,512]{2,1,0:T(8,128)(2,1)S(1)}, u32[]{:S(2)}, u32[]{:S(2)}) collective-permute-start(bf16[2,128,512]{2,1,0:T(8,128)(2,1)S(1)} %shard_map.65), channel_id=1, source_target_pairs={{0,112},{4,116},{8,120},{12,124},{16,0},{20,4},{24,8},{28,12},{32,... | collective-permute-start | bytes 786440 | tf_op jit(solution)/shard_map/ppermute | solution.py:226
  21.2 17.3 %collective-permute-start.2 = (bf16[2,128,512]{2,1,0:T(8,128)(2,1)S(1)}, bf16[2,128,512]{2,1,0:T(8,128)(2,1)S(1)}, u32[]{:S(2)}, u32[]{:S(2)}) collective-permute-start(bf16[2,128,512]{2,1,0:T(8,128)(2,1)S(1)} %collective-permute-done.1.x), channel_id=1, source_target_pairs={{0,4},{4,0},{8,12},{12,8},{16,20},{20,16},{24,28},{28,24},{32,36},... | collective-permute-start | bytes 786440 | tf_op jit(solution)/shard_map/ppermute | solution.py:197
  30.6 8.6 %collective-permute-start.44 = (bf16[128,512]{1,0:T(8,128)(2,1)S(1)}, bf16[128,512]{1,0:T(8,128)(2,1)S(1)}, u32[]{:S(2)}, u32[]{:S(2)}) collective-permute-start(bf16[128,512]{1,0:T(8,128)(2,1)S(1)} %slice_bitcast_fusion.5), channel_id=1, source_target_pairs={{0,4},{4,0},{8,12},{12,8},{16,20},{20,16},{24,28},{28,24},{32,36},... | collective-permute-start | bytes 393224 | tf_op jit(solution)/shard_map/ppermute | solution.py:197
  30.8 23.1 %collective-permute-start.7 = (f32[512]{0:T(512)S(1)}, f32[512]{0:T(512)S(1)}, u32[]{:S(2)}, u32[]{:S(2)}) collective-permute-start(f32[512]{0:T(512)S(1)} %bitcast.73), channel_id=1, source_target_pairs={{0,112},{4,116},{8,120},{12,124},{16,0},{20,4},{24,8},{28,12},{32,... | collective-permute-start | bytes 6152 | tf_op jit(solution)/shard_map/ppermute | solution.py:229
  39.3 6.4 %collective-permute-start.46 = (bf16[128,512]{1,0:T(8,128)(2,1)S(1)}, bf16[128,512]{1,0:T(8,128)(2,1)S(1)}, u32[]{:S(2)}, u32[]{:S(2)}) collective-permute-start(bf16[128,512]{1,0:T(8,128)(2,1)S(1)} %shard_map.93.x0), channel_id=1, source_target_pairs={{0,3},{1,0},{2,1},{3,2},{16,19},{17,16},{18,17},{19,18},{32,35},{3... | collective-permute-start | bytes 393224 | tf_op jit(solution)/shard_map/ppermute | solution.py:212
  40.3 7.9 %collective-permute-start.47 = (bf16[128,512]{1,0:T(8,128)(2,1)S(1)}, bf16[128,512]{1,0:T(8,128)(2,1)S(1)}, u32[]{:S(2)}, u32[]{:S(2)}) collective-permute-start(bf16[128,512]{1,0:T(8,128)(2,1)S(1)} %shard_map.93.x0), channel_id=1, source_target_pairs={{0,2},{1,3},{2,0},{3,1},{16,18},{17,19},{18,16},{19,17},{32,34},{3... | collective-permute-start | bytes 393224 | tf_op jit(solution)/shard_map/ppermute | solution.py:212
  41.3 8.6 %collective-permute-start.45 = (bf16[128,512]{1,0:T(8,128)(2,1)S(1)}, bf16[128,512]{1,0:T(8,128)(2,1)S(1)}, u32[]{:S(2)}, u32[]{:S(2)}) collective-permute-start(bf16[128,512]{1,0:T(8,128)(2,1)S(1)} %shard_map.93.x0), channel_id=1, source_target_pairs={{0,1},{1,2},{2,3},{3,0},{16,17},{17,18},{18,19},{19,16},{32,33},{3... | collective-permute-start | bytes 393224 | tf_op jit(solution)/shard_map/ppermute | solution.py:212
  45.8 8.2 %collective-permute-start.3 = (bf16[128,512]{1,0:T(8,128)(2,1)S(1)}, bf16[128,512]{1,0:T(8,128)(2,1)S(1)}, u32[]{:S(2)}, u32[]{:S(2)}) collective-permute-start(bf16[128,512]{1,0:T(8,128)(2,1)S(1)} %get-tuple-element.47), channel_id=1, source_target_pairs={{0,1},{1,2},{2,3},{3,0},{16,17},{17,18},{18,19},{19,16},{32,33},{3... | collective-permute-start | bytes 393224 | tf_op jit(solution)/shard_map/ppermute | solution.py:212
  48.2 7.0 %collective-permute-start.4 = (bf16[128,512]{1,0:T(8,128)(2,1)S(1)}, bf16[128,512]{1,0:T(8,128)(2,1)S(1)}, u32[]{:S(2)}, u32[]{:S(2)}) collective-permute-start(bf16[128,512]{1,0:T(8,128)(2,1)S(1)} %get-tuple-element.46), channel_id=1, source_target_pairs={{0,2},{1,3},{2,0},{3,1},{16,18},{17,19},{18,16},{19,17},{32,34},{3... | collective-permute-start | bytes 393224 | tf_op jit(solution)/shard_map/ppermute | solution.py:212
  49.9 6.0 %collective-permute-start.5 = (bf16[128,512]{1,0:T(8,128)(2,1)S(1)}, bf16[128,512]{1,0:T(8,128)(2,1)S(1)}, u32[]{:S(2)}, u32[]{:S(2)}) collective-permute-start(bf16[128,512]{1,0:T(8,128)(2,1)S(1)} %get-tuple-element.45), channel_id=1, source_target_pairs={{0,3},{1,0},{2,1},{3,2},{16,19},{17,16},{18,17},{19,18},{32,35},{3... | collective-permute-start | bytes 393224 | tf_op jit(solution)/shard_map/ppermute | solution.py:212
  53.8 4.4 %collective-permute-start.48 = (bf16[2,128,512]{2,1,0:T(8,128)(2,1)S(1)}, bf16[2,128,512]{2,1,0:T(8,128)(2,1)S(1)}, u32[]{:S(2)}, u32[]{:S(2)}) collective-permute-start(bf16[2,128,512]{2,1,0:T(8,128)(2,1)S(1)} %get-tuple-element.21), channel_id=1, source_target_pairs={{0,4},{4,0},{8,12},{12,8},{16,20},{20,16},{24,28},{28,24},{32,36},... | collective-permute-start | bytes 786440 | tf_op jit(solution)/shard_map/ppermute | solution.py:197
  57.5 9.7 %collective-permute-start.9 = (bf16[2,128,512]{2,1,0:T(8,128)(2,1)S(1)}, bf16[2,128,512]{2,1,0:T(8,128)(2,1)S(1)}, u32[]{:S(2)}, u32[]{:S(2)}) collective-permute-start(bf16[2,128,512]{2,1,0:T(8,128)(2,1)S(1)} %shard_map.67), channel_id=1, source_target_pairs={{112,0},{116,12},{120,8},{124,4},{0,16},{4,28},{8,24},{12,20},{16,... | collective-permute-start | bytes 786440 | tf_op jit(solution)/shard_map/ppermute | solution.py:204
  58.3 9.5 %collective-permute-start.49 = (bf16[2,128,512]{2,1,0:T(8,128)(2,1)S(1)}, bf16[2,128,512]{2,1,0:T(8,128)(2,1)S(1)}, u32[]{:S(2)}, u32[]{:S(2)}) collective-permute-start(bf16[2,128,512]{2,1,0:T(8,128)(2,1)S(1)} %shard_map.97), channel_id=1, source_target_pairs={{0,112},{4,124},{8,120},{12,116},{16,0},{20,12},{24,8},{28,4},{32,... | collective-permute-start | bytes 786440 | tf_op jit(solution)/shard_map/ppermute | solution.py:204
  70.3 11.4 %collective-permute-start.52 = (bf16[128,512]{1,0:T(8,128)(2,1)S(1)}, bf16[128,512]{1,0:T(8,128)(2,1)S(1)}, u32[]{:S(2)}, u32[]{:S(2)}) collective-permute-start(bf16[128,512]{1,0:T(8,128)(2,1)S(1)} %shard_map.98.x0), channel_id=1, source_target_pairs={{0,3},{1,0},{2,1},{3,2},{16,19},{17,16},{18,17},{19,18},{32,35},{3... | collective-permute-start | bytes 393224 | tf_op jit(solution)/shard_map/ppermute | solution.py:212
  73.2 12.2 %collective-permute-start.53 = (bf16[128,512]{1,0:T(8,128)(2,1)S(1)}, bf16[128,512]{1,0:T(8,128)(2,1)S(1)}, u32[]{:S(2)}, u32[]{:S(2)}) collective-permute-start(bf16[128,512]{1,0:T(8,128)(2,1)S(1)} %shard_map.98.x0), channel_id=1, source_target_pairs={{0,2},{1,3},{2,0},{3,1},{16,18},{17,19},{18,16},{19,17},{32,34},{3... | collective-permute-start | bytes 393224 | tf_op jit(solution)/shard_map/ppermute | solution.py:212
  73.2 13.1 %collective-permute-start.51 = (bf16[128,512]{1,0:T(8,128)(2,1)S(1)}, bf16[128,512]{1,0:T(8,128)(2,1)S(1)}, u32[]{:S(2)}, u32[]{:S(2)}) collective-permute-start(bf16[128,512]{1,0:T(8,128)(2,1)S(1)} %shard_map.98.x0), channel_id=1, source_target_pairs={{0,1},{1,2},{2,3},{3,0},{16,17},{17,18},{18,19},{19,16},{32,33},{3... | collective-permute-start | bytes 393224 | tf_op jit(solution)/shard_map/ppermute | solution.py:212
  74.2 12.7 %collective-permute-start.11 = (bf16[128,512]{1,0:T(8,128)(2,1)S(1)}, bf16[128,512]{1,0:T(8,128)(2,1)S(1)}, u32[]{:S(2)}, u32[]{:S(2)}) collective-permute-start(bf16[128,512]{1,0:T(8,128)(2,1)S(1)} %get-tuple-element.44), channel_id=1, source_target_pairs={{0,1},{1,2},{2,3},{3,0},{16,17},{17,18},{18,19},{19,16},{32,33},{3... | collective-permute-start | bytes 393224 | tf_op jit(solution)/shard_map/ppermute | solution.py:212
  76.8 11.5 %collective-permute-start.12 = (bf16[128,512]{1,0:T(8,128)(2,1)S(1)}, bf16[128,512]{1,0:T(8,128)(2,1)S(1)}, u32[]{:S(2)}, u32[]{:S(2)}) collective-permute-start(bf16[128,512]{1,0:T(8,128)(2,1)S(1)} %get-tuple-element.43), channel_id=1, source_target_pairs={{0,2},{1,3},{2,0},{3,1},{16,18},{17,19},{18,16},{19,17},{32,34},{3... | collective-permute-start | bytes 393224 | tf_op jit(solution)/shard_map/ppermute | solution.py:212
  81.7 6.6 %collective-permute-start.13 = (bf16[128,512]{1,0:T(8,128)(2,1)S(1)}, bf16[128,512]{1,0:T(8,128)(2,1)S(1)}, u32[]{:S(2)}, u32[]{:S(2)}) collective-permute-start(bf16[128,512]{1,0:T(8,128)(2,1)S(1)} %get-tuple-element.42), channel_id=1, source_target_pairs={{0,3},{1,0},{2,1},{3,2},{16,19},{17,16},{18,17},{19,18},{32,35},{3... | collective-permute-start | bytes 393224 | tf_op jit(solution)/shard_map/ppermute | solution.py:212
  86.8 5.9 %collective-permute-start.54 = (bf16[2,128,512]{2,1,0:T(8,128)(2,1)S(1)}, bf16[2,128,512]{2,1,0:T(8,128)(2,1)S(1)}, u32[]{:S(2)}, u32[]{:S(2)}) collective-permute-start(bf16[2,128,512]{2,1,0:T(8,128)(2,1)S(1)} %get-tuple-element.23), channel_id=1, source_target_pairs={{0,4},{4,0},{8,12},{12,8},{16,20},{20,16},{24,28},{28,24},{32,36},... | collective-permute-start | bytes 786440 | tf_op jit(solution)/shard_map/ppermute | solution.py:197
  89.9 10.1 %collective-permute-start.15 = (bf16[2,128,512]{2,1,0:T(8,128)(2,1)S(1)}, bf16[2,128,512]{2,1,0:T(8,128)(2,1)S(1)}, u32[]{:S(2)}, u32[]{:S(2)}) collective-permute-start(bf16[2,128,512]{2,1,0:T(8,128)(2,1)S(1)} %shard_map.71), channel_id=1, source_target_pairs={{112,0},{116,12},{120,8},{124,4},{0,16},{4,28},{8,24},{12,20},{16,... | collective-permute-start | bytes 786440 | tf_op jit(solution)/shard_map/ppermute | solution.py:204
  92.8 8.3 %collective-permute-start.55 = (bf16[2,128,512]{2,1,0:T(8,128)(2,1)S(1)}, bf16[2,128,512]{2,1,0:T(8,128)(2,1)S(1)}, u32[]{:S(2)}, u32[]{:S(2)}) collective-permute-start(bf16[2,128,512]{2,1,0:T(8,128)(2,1)S(1)} %shard_map.102), channel_id=1, source_target_pairs={{0,112},{4,124},{8,120},{12,116},{16,0},{20,12},{24,8},{28,4},{32,... | collective-permute-start | bytes 786440 | tf_op jit(solution)/shard_map/ppermute | solution.py:204
  100.0 5.0 %collective-permute-start.16 = (bf16[2,128,512]{2,1,0:T(8,128)(2,1)S(1)}, bf16[2,128,512]{2,1,0:T(8,128)(2,1)S(1)}, u32[]{:S(2)}, u32[]{:S(2)}) collective-permute-start(bf16[2,128,512]{2,1,0:T(8,128)(2,1)S(1)} %collective-permute-done.15.x), channel_id=1, source_target_pairs={{0,4},{4,0},{8,12},{12,8},{16,20},{20,16},{24,28},{28,24},{32,36},... | collective-permute-start | bytes 786440 | tf_op jit(solution)/shard_map/ppermute | solution.py:197
  101.0 4.7 %collective-permute-start.56 = (bf16[128,512]{1,0:T(8,128)(2,1)S(1)}, bf16[128,512]{1,0:T(8,128)(2,1)S(1)}, u32[]{:S(2)}, u32[]{:S(2)}) collective-permute-start(bf16[128,512]{1,0:T(8,128)(2,1)S(1)} %slice_bitcast_fusion.3), channel_id=1, source_target_pairs={{0,4},{4,0},{8,12},{12,8},{16,20},{20,16},{24,28},{28,24},{32,36},... | collective-permute-start | bytes 393224 | tf_op jit(solution)/shard_map/ppermute | solution.py:197
  102.3 18.1 %collective-permute-start.20 = (bf16[3,128,512]{2,1,0:T(8,128)(2,1)S(1)}, bf16[3,128,512]{2,1,0:T(8,128)(2,1)S(1)}, u32[]{:S(2)}, u32[]{:S(2)}) collective-permute-start(bf16[3,128,512]{2,1,0:T(8,128)(2,1)S(1)} %shard_map.74), channel_id=1, source_target_pairs={{0,112},{4,116},{8,120},{12,124},{16,0},{20,4},{24,8},{28,12},{32,... | collective-permute-start | bytes 1179656 | tf_op jit(solution)/shard_map/ppermute | solution.py:228
  105.9 9.3 %collective-permute-start.58 = (bf16[128,512]{1,0:T(8,128)(2,1)S(1)}, bf16[128,512]{1,0:T(8,128)(2,1)S(1)}, u32[]{:S(2)}, u32[]{:S(2)}) collective-permute-start(bf16[128,512]{1,0:T(8,128)(2,1)S(1)} %shard_map.103.x0), channel_id=1, source_target_pairs={{0,3},{1,0},{2,1},{3,2},{16,19},{17,16},{18,17},{19,18},{32,35},{3... | collective-permute-start | bytes 393224 | tf_op jit(solution)/shard_map/ppermute | solution.py:212
  109.2 7.9 %collective-permute-start.59 = (bf16[128,512]{1,0:T(8,128)(2,1)S(1)}, bf16[128,512]{1,0:T(8,128)(2,1)S(1)}, u32[]{:S(2)}, u32[]{:S(2)}) collective-permute-start(bf16[128,512]{1,0:T(8,128)(2,1)S(1)} %shard_map.103.x0), channel_id=1, source_target_pairs={{0,2},{1,3},{2,0},{3,1},{16,18},{17,19},{18,16},{19,17},{32,34},{3... | collective-permute-start | bytes 393224 | tf_op jit(solution)/shard_map/ppermute | solution.py:212
  109.2 10.6 %collective-permute-start.57 = (bf16[128,512]{1,0:T(8,128)(2,1)S(1)}, bf16[128,512]{1,0:T(8,128)(2,1)S(1)}, u32[]{:S(2)}, u32[]{:S(2)}) collective-permute-start(bf16[128,512]{1,0:T(8,128)(2,1)S(1)} %shard_map.103.x0), channel_id=1, source_target_pairs={{0,1},{1,2},{2,3},{3,0},{16,17},{17,18},{18,19},{19,16},{32,33},{3... | collective-permute-start | bytes 393224 | tf_op jit(solution)/shard_map/ppermute | solution.py:212
  110.2 11.8 %collective-permute-start.17 = (bf16[128,512]{1,0:T(8,128)(2,1)S(1)}, bf16[128,512]{1,0:T(8,128)(2,1)S(1)}, u32[]{:S(2)}, u32[]{:S(2)}) collective-permute-start(bf16[128,512]{1,0:T(8,128)(2,1)S(1)} %get-tuple-element.41), channel_id=1, source_target_pairs={{0,1},{1,2},{2,3},{3,0},{16,17},{17,18},{18,19},{19,16},{32,33},{3... | collective-permute-start | bytes 393224 | tf_op jit(solution)/shard_map/ppermute | solution.py:212
  115.2 9.4 %collective-permute-start.18 = (bf16[128,512]{1,0:T(8,128)(2,1)S(1)}, bf16[128,512]{1,0:T(8,128)(2,1)S(1)}, u32[]{:S(2)}, u32[]{:S(2)}) collective-permute-start(bf16[128,512]{1,0:T(8,128)(2,1)S(1)} %get-tuple-element.40), channel_id=1, source_target_pairs={{0,2},{1,3},{2,0},{3,1},{16,18},{17,19},{18,16},{19,17},{32,34},{3... | collective-permute-start | bytes 393224 | tf_op jit(solution)/shard_map/ppermute | solution.py:212
  117.1 8.4 %collective-permute-start.19 = (bf16[128,512]{1,0:T(8,128)(2,1)S(1)}, bf16[128,512]{1,0:T(8,128)(2,1)S(1)}, u32[]{:S(2)}, u32[]{:S(2)}) collective-permute-start(bf16[128,512]{1,0:T(8,128)(2,1)S(1)} %get-tuple-element.39), channel_id=1, source_target_pairs={{0,3},{1,0},{2,1},{3,2},{16,19},{17,16},{18,17},{19,18},{32,35},{3... | collective-permute-start | bytes 393224 | tf_op jit(solution)/shard_map/ppermute | solution.py:212
  120.2 10.5 %collective-permute-start.60 = (bf16[2,128,512]{2,1,0:T(8,128)(2,1)S(1)}, bf16[2,128,512]{2,1,0:T(8,128)(2,1)S(1)}, u32[]{:S(2)}, u32[]{:S(2)}) collective-permute-start(bf16[2,128,512]{2,1,0:T(8,128)(2,1)S(1)} %get-tuple-element.25), channel_id=1, source_target_pairs={{0,4},{4,0},{8,12},{12,8},{16,20},{20,16},{24,28},{28,24},{32,36},... | collective-permute-start | bytes 786440 | tf_op jit(solution)/shard_map/ppermute | solution.py:197
  127.1 9.2 %collective-permute-start.22 = (bf16[2,128,512]{2,1,0:T(8,128)(2,1)S(1)}, bf16[2,128,512]{2,1,0:T(8,128)(2,1)S(1)}, u32[]{:S(2)}, u32[]{:S(2)}) collective-permute-start(bf16[2,128,512]{2,1,0:T(8,128)(2,1)S(1)} %shard_map.76), channel_id=1, source_target_pairs={{112,0},{116,12},{120,8},{124,4},{0,16},{4,28},{8,24},{12,20},{16,... | collective-permute-start | bytes 786440 | tf_op jit(solution)/shard_map/ppermute | solution.py:204
  130.7 8.1 %collective-permute-start.61 = (bf16[2,128,512]{2,1,0:T(8,128)(2,1)S(1)}, bf16[2,128,512]{2,1,0:T(8,128)(2,1)S(1)}, u32[]{:S(2)}, u32[]{:S(2)}) collective-permute-start(bf16[2,128,512]{2,1,0:T(8,128)(2,1)S(1)} %shard_map.107), channel_id=1, source_target_pairs={{0,112},{4,124},{8,120},{12,116},{16,0},{20,12},{24,8},{28,4},{32,... | collective-permute-start | bytes 786440 | tf_op jit(solution)/shard_map/ppermute | solution.py:204
  136.3 3.8 %collective-permute-start.23 = (bf16[2,128,512]{2,1,0:T(8,128)(2,1)S(1)}, bf16[2,128,512]{2,1,0:T(8,128)(2,1)S(1)}, u32[]{:S(2)}, u32[]{:S(2)}) collective-permute-start(bf16[2,128,512]{2,1,0:T(8,128)(2,1)S(1)} %collective-permute-done.22.x), channel_id=1, source_target_pairs={{0,4},{4,0},{8,12},{12,8},{16,20},{20,16},{24,28},{28,24},{32,36},... | collective-permute-start | bytes 786440 | tf_op jit(solution)/shard_map/ppermute | solution.py:197
  140.9 11.3 %collective-permute-start.64 = (bf16[128,512]{1,0:T(8,128)(2,1)S(1)}, bf16[128,512]{1,0:T(8,128)(2,1)S(1)}, u32[]{:S(2)}, u32[]{:S(2)}) collective-permute-start(bf16[128,512]{1,0:T(8,128)(2,1)S(1)} %shard_map.108.x0), channel_id=1, source_target_pairs={{0,3},{1,0},{2,1},{3,2},{16,19},{17,16},{18,17},{19,18},{32,35},{3... | collective-permute-start | bytes 393224 | tf_op jit(solution)/shard_map/ppermute | solution.py:212
  143.3 12.5 %collective-permute-start.65 = (bf16[128,512]{1,0:T(8,128)(2,1)S(1)}, bf16[128,512]{1,0:T(8,128)(2,1)S(1)}, u32[]{:S(2)}, u32[]{:S(2)}) collective-permute-start(bf16[128,512]{1,0:T(8,128)(2,1)S(1)} %shard_map.108.x0), channel_id=1, source_target_pairs={{0,2},{1,3},{2,0},{3,1},{16,18},{17,19},{18,16},{19,17},{32,34},{3... | collective-permute-start | bytes 393224 | tf_op jit(solution)/shard_map/ppermute | solution.py:212
  143.3 13.4 %collective-permute-start.63 = (bf16[128,512]{1,0:T(8,128)(2,1)S(1)}, bf16[128,512]{1,0:T(8,128)(2,1)S(1)}, u32[]{:S(2)}, u32[]{:S(2)}) collective-permute-start(bf16[128,512]{1,0:T(8,128)(2,1)S(1)} %shard_map.108.x0), channel_id=1, source_target_pairs={{0,1},{1,2},{2,3},{3,0},{16,17},{17,18},{18,19},{19,16},{32,33},{3... | collective-permute-start | bytes 393224 | tf_op jit(solution)/shard_map/ppermute | solution.py:212
  144.5 12.8 %collective-permute-start.24 = (bf16[128,512]{1,0:T(8,128)(2,1)S(1)}, bf16[128,512]{1,0:T(8,128)(2,1)S(1)}, u32[]{:S(2)}, u32[]{:S(2)}) collective-permute-start(bf16[128,512]{1,0:T(8,128)(2,1)S(1)} %get-tuple-element.38), channel_id=1, source_target_pairs={{0,1},{1,2},{2,3},{3,0},{16,17},{17,18},{18,19},{19,16},{32,33},{3... | collective-permute-start | bytes 393224 | tf_op jit(solution)/shard_map/ppermute | solution.py:212
  146.9 11.8 %collective-permute-start.25 = (bf16[128,512]{1,0:T(8,128)(2,1)S(1)}, bf16[128,512]{1,0:T(8,128)(2,1)S(1)}, u32[]{:S(2)}, u32[]{:S(2)}) collective-permute-start(bf16[128,512]{1,0:T(8,128)(2,1)S(1)} %get-tuple-element.37), channel_id=1, source_target_pairs={{0,2},{1,3},{2,0},{3,1},{16,18},{17,19},{18,16},{19,17},{32,34},{3... | collective-permute-start | bytes 393224 | tf_op jit(solution)/shard_map/ppermute | solution.py:212
  152.1 6.5 %collective-permute-start.26 = (bf16[128,512]{1,0:T(8,128)(2,1)S(1)}, bf16[128,512]{1,0:T(8,128)(2,1)S(1)}, u32[]{:S(2)}, u32[]{:S(2)}) collective-permute-start(bf16[128,512]{1,0:T(8,128)(2,1)S(1)} %get-tuple-element.36), channel_id=1, source_target_pairs={{0,3},{1,0},{2,1},{3,2},{16,19},{17,16},{18,17},{19,18},{32,35},{3... | collective-permute-start | bytes 393224 | tf_op jit(solution)/shard_map/ppermute | solution.py:212
  157.2 7.6 %collective-permute-start.66 = (bf16[2,128,512]{2,1,0:T(8,128)(2,1)S(1)}, bf16[2,128,512]{2,1,0:T(8,128)(2,1)S(1)}, u32[]{:S(2)}, u32[]{:S(2)}) collective-permute-start(bf16[2,128,512]{2,1,0:T(8,128)(2,1)S(1)} %get-tuple-element.27), channel_id=1, source_target_pairs={{0,4},{4,0},{8,12},{12,8},{16,20},{20,16},{24,28},{28,24},{32,36},... | collective-permute-start | bytes 786440 | tf_op jit(solution)/shard_map/ppermute | solution.py:197
  160.2 9.0 %collective-permute-start.28 = (bf16[2,128,512]{2,1,0:T(8,128)(2,1)S(1)}, bf16[2,128,512]{2,1,0:T(8,128)(2,1)S(1)}, u32[]{:S(2)}, u32[]{:S(2)}) collective-permute-start(bf16[2,128,512]{2,1,0:T(8,128)(2,1)S(1)} %shard_map.80), channel_id=1, source_target_pairs={{112,0},{116,12},{120,8},{124,4},{0,16},{4,28},{8,24},{12,20},{16,... | collective-permute-start | bytes 786440 | tf_op jit(solution)/shard_map/ppermute | solution.py:204
  164.8 7.2 %collective-permute-start.67 = (bf16[2,128,512]{2,1,0:T(8,128)(2,1)S(1)}, bf16[2,128,512]{2,1,0:T(8,128)(2,1)S(1)}, u32[]{:S(2)}, u32[]{:S(2)}) collective-permute-start(bf16[2,128,512]{2,1,0:T(8,128)(2,1)S(1)} %shard_map.112), channel_id=1, source_target_pairs={{0,112},{4,124},{8,120},{12,116},{16,0},{20,12},{24,8},{28,4},{32,... | collective-permute-start | bytes 786440 | tf_op jit(solution)/shard_map/ppermute | solution.py:204
  169.3 4.6 %collective-permute-start.29 = (bf16[2,128,512]{2,1,0:T(8,128)(2,1)S(1)}, bf16[2,128,512]{2,1,0:T(8,128)(2,1)S(1)}, u32[]{:S(2)}, u32[]{:S(2)}) collective-permute-start(bf16[2,128,512]{2,1,0:T(8,128)(2,1)S(1)} %collective-permute-done.28.x), channel_id=1, source_target_pairs={{0,4},{4,0},{8,12},{12,8},{16,20},{20,16},{24,28},{28,24},{32,36},... | collective-permute-start | bytes 786440 | tf_op jit(solution)/shard_map/ppermute | solution.py:197
  174.7 12.1 %collective-permute-start.70 = (bf16[128,512]{1,0:T(8,128)(2,1)S(1)}, bf16[128,512]{1,0:T(8,128)(2,1)S(1)}, u32[]{:S(2)}, u32[]{:S(2)}) collective-permute-start(bf16[128,512]{1,0:T(8,128)(2,1)S(1)} %shard_map.113.x0), channel_id=1, source_target_pairs={{0,3},{1,0},{2,1},{3,2},{16,19},{17,16},{18,17},{19,18},{32,35},{3... | collective-permute-start | bytes 393224 | tf_op jit(solution)/shard_map/ppermute | solution.py:212
  178.2 13.2 %collective-permute-start.71 = (bf16[128,512]{1,0:T(8,128)(2,1)S(1)}, bf16[128,512]{1,0:T(8,128)(2,1)S(1)}, u32[]{:S(2)}, u32[]{:S(2)}) collective-permute-start(bf16[128,512]{1,0:T(8,128)(2,1)S(1)} %shard_map.113.x0), channel_id=1, source_target_pairs={{0,2},{1,3},{2,0},{3,1},{16,18},{17,19},{18,16},{19,17},{32,34},{3... | collective-permute-start | bytes 393224 | tf_op jit(solution)/shard_map/ppermute | solution.py:212
  178.2 14.1 %collective-permute-start.69 = (bf16[128,512]{1,0:T(8,128)(2,1)S(1)}, bf16[128,512]{1,0:T(8,128)(2,1)S(1)}, u32[]{:S(2)}, u32[]{:S(2)}) collective-permute-start(bf16[128,512]{1,0:T(8,128)(2,1)S(1)} %shard_map.113.x0), channel_id=1, source_target_pairs={{0,1},{1,2},{2,3},{3,0},{16,17},{17,18},{18,19},{19,16},{32,33},{3... | collective-permute-start | bytes 393224 | tf_op jit(solution)/shard_map/ppermute | solution.py:212
  179.2 13.7 %collective-permute-start.30 = (bf16[128,512]{1,0:T(8,128)(2,1)S(1)}, bf16[128,512]{1,0:T(8,128)(2,1)S(1)}, u32[]{:S(2)}, u32[]{:S(2)}) collective-permute-start(bf16[128,512]{1,0:T(8,128)(2,1)S(1)} %get-tuple-element.35), channel_id=1, source_target_pairs={{0,1},{1,2},{2,3},{3,0},{16,17},{17,18},{18,19},{19,16},{32,33},{3... | collective-permute-start | bytes 393224 | tf_op jit(solution)/shard_map/ppermute | solution.py:212
  181.8 11.5 %collective-permute-start.31 = (bf16[128,512]{1,0:T(8,128)(2,1)S(1)}, bf16[128,512]{1,0:T(8,128)(2,1)S(1)}, u32[]{:S(2)}, u32[]{:S(2)}) collective-permute-start(bf16[128,512]{1,0:T(8,128)(2,1)S(1)} %get-tuple-element.34), channel_id=1, source_target_pairs={{0,2},{1,3},{2,0},{3,1},{16,18},{17,19},{18,16},{19,17},{32,34},{3... | collective-permute-start | bytes 393224 | tf_op jit(solution)/shard_map/ppermute | solution.py:212
  186.8 6.6 %collective-permute-start.32 = (bf16[128,512]{1,0:T(8,128)(2,1)S(1)}, bf16[128,512]{1,0:T(8,128)(2,1)S(1)}, u32[]{:S(2)}, u32[]{:S(2)}) collective-permute-start(bf16[128,512]{1,0:T(8,128)(2,1)S(1)} %get-tuple-element.33), channel_id=1, source_target_pairs={{0,3},{1,0},{2,1},{3,2},{16,19},{17,16},{18,17},{19,18},{32,35},{3... | collective-permute-start | bytes 393224 | tf_op jit(solution)/shard_map/ppermute | solution.py:212
  192.8 7.7 %collective-permute-start.72 = (bf16[2,128,512]{2,1,0:T(8,128)(2,1)S(1)}, bf16[2,128,512]{2,1,0:T(8,128)(2,1)S(1)}, u32[]{:S(2)}, u32[]{:S(2)}) collective-permute-start(bf16[2,128,512]{2,1,0:T(8,128)(2,1)S(1)} %get-tuple-element.29), channel_id=1, source_target_pairs={{0,4},{4,0},{8,12},{12,8},{16,20},{20,16},{24,28},{28,24},{32,36},... | collective-permute-start | bytes 786440 | tf_op jit(solution)/shard_map/ppermute | solution.py:197
  194.9 9.5 %collective-permute-start.34 = (bf16[2,128,512]{2,1,0:T(8,128)(2,1)S(1)}, bf16[2,128,512]{2,1,0:T(8,128)(2,1)S(1)}, u32[]{:S(2)}, u32[]{:S(2)}) collective-permute-start(bf16[2,128,512]{2,1,0:T(8,128)(2,1)S(1)} %shard_map.84), channel_id=1, source_target_pairs={{112,0},{116,12},{120,8},{124,4},{0,16},{4,28},{8,24},{12,20},{16,... | collective-permute-start | bytes 786440 | tf_op jit(solution)/shard_map/ppermute | solution.py:204
  200.5 5.5 %collective-permute-start.73 = (bf16[2,128,512]{2,1,0:T(8,128)(2,1)S(1)}, bf16[2,128,512]{2,1,0:T(8,128)(2,1)S(1)}, u32[]{:S(2)}, u32[]{:S(2)}) collective-permute-start(bf16[2,128,512]{2,1,0:T(8,128)(2,1)S(1)} %shard_map.117), channel_id=1, source_target_pairs={{0,0},{4,12},{8,8},{12,4},{16,16},{20,28},{24,24},{28,20},{32,32},... | collective-permute-start | bytes 786440 | tf_op jit(solution)/shard_map/ppermute | solution.py:208
  204.3 5.9 %collective-permute-start.35 = (bf16[2,128,512]{2,1,0:T(8,128)(2,1)S(1)}, bf16[2,128,512]{2,1,0:T(8,128)(2,1)S(1)}, u32[]{:S(2)}, u32[]{:S(2)}) collective-permute-start(bf16[2,128,512]{2,1,0:T(8,128)(2,1)S(1)} %collective-permute-done.34.x), channel_id=1, source_target_pairs={{0,4},{4,0},{8,12},{12,8},{16,20},{20,16},{24,28},{28,24},{32,36},... | collective-permute-start | bytes 786440 | tf_op jit(solution)/shard_map/ppermute | solution.py:197
  206.1 9.8 %collective-permute-start.74 = (bf16[128,512]{1,0:T(8,128)(2,1)S(1)}, bf16[128,512]{1,0:T(8,128)(2,1)S(1)}, u32[]{:S(2)}, u32[]{:S(2)}) collective-permute-start(bf16[128,512]{1,0:T(8,128)(2,1)S(1)} %slice_bitcast_fusion), channel_id=1, source_target_pairs={{0,4},{4,0},{8,12},{12,8},{16,20},{20,16},{24,28},{28,24},{32,36},... | collective-permute-start | bytes 393224 | tf_op jit(solution)/shard_map/ppermute | solution.py:197
  211.0 7.1 %collective-permute-start.36 = (bf16[128,512]{1,0:T(8,128)(2,1)S(1)}, bf16[128,512]{1,0:T(8,128)(2,1)S(1)}, u32[]{:S(2)}, u32[]{:S(2)}) collective-permute-start(bf16[128,512]{1,0:T(8,128)(2,1)S(1)} %get-tuple-element.32), channel_id=1, source_target_pairs={{0,1},{1,2},{2,3},{3,0},{16,17},{17,18},{18,19},{19,16},{32,33},{3... | collective-permute-start | bytes 393224 | tf_op jit(solution)/shard_map/ppermute | solution.py:212
  211.1 11.0 %collective-permute-start.37 = (bf16[128,512]{1,0:T(8,128)(2,1)S(1)}, bf16[128,512]{1,0:T(8,128)(2,1)S(1)}, u32[]{:S(2)}, u32[]{:S(2)}) collective-permute-start(bf16[128,512]{1,0:T(8,128)(2,1)S(1)} %get-tuple-element.31), channel_id=1, source_target_pairs={{0,2},{1,3},{2,0},{3,1},{16,18},{17,19},{18,16},{19,17},{32,34},{3... | collective-permute-start | bytes 393224 | tf_op jit(solution)/shard_map/ppermute | solution.py:212
  215.8 6.2 %collective-permute-start.38 = (bf16[128,512]{1,0:T(8,128)(2,1)S(1)}, bf16[128,512]{1,0:T(8,128)(2,1)S(1)}, u32[]{:S(2)}, u32[]{:S(2)}) collective-permute-start(bf16[128,512]{1,0:T(8,128)(2,1)S(1)} %get-tuple-element.30), channel_id=1, source_target_pairs={{0,3},{1,0},{2,1},{3,2},{16,19},{17,16},{18,17},{19,18},{32,35},{3... | collective-permute-start | bytes 393224 | tf_op jit(solution)/shard_map/ppermute | solution.py:212
  (16 other events, 53.8 us)
